TPU v7x, 32 devices: a whole 2x2x4 slice. The times are simulated.
32 devices in a mesh: page: 8 (over z, x), head: 4 (over y, core).
Axes of the slice: x: 2, y: 2, z: 4, core: 2. Of those that a mesh axis runs over, the one named last changes fastest.
Arguments:
- tokens: bfloat16 [2, 2, 4096, 768], P(None, None, ('page', 'head')), may hold values from -6 to 6
- spatial: bfloat16 [2, 2, 4096, 768], P(None, None, ('page', 'head')), may hold values from -6 to 6
- box_coords: int32 [2, 2, 2, 4096], P(None, None, None, 'page'), may hold values from 0 to 1023
- reading_order: int32 [2, 2, 4096], P(None, None, 'page'), may hold values from 0 to 127
- page_len: int32 [2, 8], P(None, 'page'), may hold values from 256 to 512, as said below
- w_attn: bfloat16 [2, 5, 768, 768], P(None, None, 'page', 'head'), may hold values from -0.21875 to 0.21875
- tables: bfloat16 [2, 3, 12, 128, 128], P(None, None, 'head', 'page'), may hold values from -3 to 3
- w_out: bfloat16 [2, 768, 768], P(None, 'head', 'page'), may hold values from -0.875 to 0.875
- ln_gain: bfloat16 [2, 768], P(None, ('page', 'head')), may hold values from 0.5 to 1.5
- ln_shift: bfloat16 [2, 768], P(None, ('page', 'head')), may hold values from -1.796875 to 1.796875
- w_up: bfloat16 [768, 3072], P(None, ('page', 'head')), may hold values from -0.21875 to 0.21875
- w_down: bfloat16 [3072, 768], P(('page', 'head')), may hold values from -0.109375 to 0.109375
- grad_out: bfloat16 [2, 4096, 768], P(None, ('page', 'head')), may hold values from -6 to 6
Outputs:
- out: bfloat16 [2, 4096, 768], P(None, ('page', 'head'))
- grad_tokens: bfloat16 [2, 2, 4096, 768], P(None, None, ('page', 'head'))
- grad_w_attn: float32 [2, 5, 768, 768], P(None, None, 'page', 'head')
- grad_tables: float32 [2, 3, 12, 128, 128], P(None, None, 'head', 'page')
- grad_w_out: float32 [2, 768, 768], P(None, 'head', 'page')
- grad_ln_gain: float32 [2, 768], P(None, ('page', 'head'))
- grad_ln_shift: float32 [2, 768], P(None, ('page', 'head'))
- grad_w_up: float32 [768, 3072], P(None, ('page', 'head'))
- grad_w_down: float32 [3072, 768], P(('page', 'head'))
Inputs may be any that keep to these rules, and one draw needn't show every extreme that they name: `page_len`: each entry is 512 (a slot with one page) or 512 / 2 (a slot with two pages); both values occur in every draw.
All inputs are finite; a program needn't handle non-finite values.
Results may differ from a plain program's by a relative error of at most 0.02.
Values may be sent and summed in bfloat16 or wider, within the bound.
No kernel may reach another device: no remote copies, remote signals or barrier semaphores. Data moves between devices by JAX's collectives and lax.ppermute only.
A program may use at most 192 MiB of HBM per device.

v0:
```python
import jax
import jax.numpy as jnp
from jax import lax
from jax.sharding import PartitionSpec as P

COORD = 1024


highest = lax.Precision.HIGHEST


def layer_norm(value, gain, shift):
    center = jnp.mean(value, axis=-1, keepdims=True)
    centred = value - center
    variance = jnp.mean(centred * centred, axis=-1, keepdims=True)
    return centred * lax.rsqrt(variance + 1e-05) * gain + shift


def exact_gelu(value):
    return jax.nn.gelu(value, approximate=False)


def one_hot(index, count):
    return (index[..., None] == jnp.arange(count, dtype=jnp.int32)).astype(jnp.bfloat16)


def fetch_weights(weight_args):
    w_attn, tables, w_out, ln_gain, ln_shift, w_up, w_down = weight_args
    attn_full, table_full, proj_own, up_full, down_full = (
        lax.all_gather(w_attn, "page", axis=2, tiled=True),
        lax.all_gather(tables, "page", axis=3, tiled=True),
        lax.all_gather(w_out, "page", axis=2, tiled=True),
        lax.all_gather(w_up, "page", axis=1, tiled=True),
        lax.all_gather(w_down, "page", axis=0, tiled=True),
    )
    gain_full, shift_full = (
        lax.all_gather(ln_gain, ("page", "head"), axis=1, tiled=True),
        lax.all_gather(ln_shift, ("page", "head"), axis=1, tiled=True),
    )
    proj_full = lax.all_gather(proj_own, "head", axis=1, tiled=True)
    return (attn_full, table_full, proj_own, proj_full, gain_full, shift_full, up_full, down_full)


def reduce_grads(grads):
    grad_attn, grad_table, grad_proj, grad_gain, grad_shift, grad_up, grad_down = grads
    attn_share, table_share, proj_share, up_share, down_share = (
        lax.psum_scatter(grad_attn, "page", scatter_dimension=2, tiled=True),
        lax.psum_scatter(grad_table, "page", scatter_dimension=3, tiled=True),
        lax.psum_scatter(grad_proj, "page", scatter_dimension=2, tiled=True),
        lax.psum_scatter(grad_up, "page", scatter_dimension=1, tiled=True),
        lax.psum_scatter(grad_down, "page", scatter_dimension=0, tiled=True),
    )
    gain_share, shift_share = (
        lax.psum_scatter(grad_gain, ("page", "head"), scatter_dimension=1, tiled=True),
        lax.psum_scatter(grad_shift, ("page", "head"), scatter_dimension=1, tiled=True),
    )
    return (attn_share, table_share, proj_share, gain_share, shift_share, up_share, down_share)


def add_up(first, second):
    if first is None:
        return second
    return tuple((left + right for left, right in zip(first, second)))


def masked_scores(per_head, pair_bias, same_page):
    score = jnp.einsum(
        "cihd,cjhd->chij", per_head[0], per_head[1], preferred_element_type=jnp.float32
    )
    score = score + jnp.einsum(
        "cihd,cjhd->chij", per_head[3], per_head[4], preferred_element_type=jnp.float32
    )
    return jnp.where(same_page[:, None], score * 0.125 + pair_bias, -1e30)


def attend_forward(rows_x, rows_s, weights, table, bucket_hot, same_page):
    slot_count, slot_len = (same_page.shape[0], same_page.shape[1])
    local_heads = table.shape[1]
    head_width = weights.shape[2]
    head_size = head_width // local_heads
    buckets = table.shape[2]
    from_tokens = jnp.einsum("gd,kde->kge", rows_x, weights[:3], preferred_element_type=jnp.float32)
    from_space = jnp.einsum("gd,kde->kge", rows_s, weights[3:], preferred_element_type=jnp.float32)
    projected = jnp.concatenate([from_tokens, from_space], axis=0).astype(jnp.bfloat16)
    per_head = projected.reshape(5, slot_count, slot_len, local_heads, head_size)
    tabled = jnp.einsum(
        "gta,thab->hgtb", bucket_hot, table, preferred_element_type=jnp.float32
    ).astype(jnp.bfloat16)
    tabled = tabled.reshape(local_heads, slot_count, slot_len, 3 * buckets)
    hot_flat = bucket_hot.reshape(slot_count, slot_len, 3 * buckets)
    pair_bias = jnp.einsum("hcib,cjb->chij", tabled, hot_flat, preferred_element_type=jnp.float32)
    masked = masked_scores(per_head, pair_bias, same_page)
    row_max = jnp.max(masked, axis=-1, keepdims=True)
    weight_exp = jnp.exp(masked - row_max)
    row_sum = jnp.sum(weight_exp, axis=-1, keepdims=True)
    attn_prob = weight_exp / row_sum
    log_total = row_max + jnp.log(row_sum)
    attended = jnp.einsum(
        "chij,cjhd->cihd",
        attn_prob.astype(jnp.bfloat16),
        per_head[2],
        preferred_element_type=jnp.float32,
    )
    head_rows = attended.astype(jnp.bfloat16).reshape(slot_count * slot_len, head_width)
    return (head_rows, (per_head, pair_bias, log_total))


def attend_backward(grad_heads, kept_state, rows_x, rows_s, weights, bucket_hot, same_page):
    per_head, pair_bias, log_total = kept_state
    slot_count, slot_len = (same_page.shape[0], same_page.shape[1])
    local_heads, head_size = (per_head.shape[3], per_head.shape[4])
    buckets = bucket_hot.shape[2]
    masked = masked_scores(per_head, pair_bias, same_page)
    attn_prob = jnp.exp(masked - log_total)
    grad_rows_heads = grad_heads.reshape(slot_count, slot_len, local_heads, head_size)
    grad_value = jnp.einsum(
        "chij,cihd->cjhd",
        attn_prob.astype(jnp.bfloat16),
        grad_rows_heads,
        preferred_element_type=jnp.float32,
    )
    grad_prob = jnp.einsum(
        "cihd,cjhd->chij", grad_rows_heads, per_head[2], preferred_element_type=jnp.float32
    )
    row_dot = jnp.sum(attn_prob * grad_prob, axis=-1, keepdims=True)
    grad_score = (attn_prob * (grad_prob - row_dot)).astype(jnp.bfloat16)
    grad_query = (
        jnp.einsum("chij,cjhd->cihd", grad_score, per_head[1], preferred_element_type=jnp.float32)
        * 0.125
    )
    grad_key = (
        jnp.einsum("chij,cihd->cjhd", grad_score, per_head[0], preferred_element_type=jnp.float32)
        * 0.125
    )
    grad_space_query = (
        jnp.einsum("chij,cjhd->cihd", grad_score, per_head[4], preferred_element_type=jnp.float32)
        * 0.125
    )
    grad_space_key = (
        jnp.einsum("chij,cihd->cjhd", grad_score, per_head[3], preferred_element_type=jnp.float32)
        * 0.125
    )
    stacked = jnp.stack(
        [grad_query, grad_key, grad_value, grad_space_query, grad_space_key]
    ).astype(jnp.bfloat16)
    stacked = stacked.reshape(5, slot_count * slot_len, local_heads * head_size)
    grad_weight = jnp.concatenate(
        [
            jnp.einsum("gd,kge->kde", rows_x, stacked[:3], preferred_element_type=jnp.float32),
            jnp.einsum("gd,kge->kde", rows_s, stacked[3:], preferred_element_type=jnp.float32),
        ],
        axis=0,
    )
    grad_rows = jnp.einsum(
        "kge,kde->gd", stacked[:3], weights[:3], preferred_element_type=jnp.float32
    )
    hot_flat = bucket_hot.reshape(slot_count, slot_len, 3 * buckets)
    spread = jnp.einsum("chij,cjb->chib", grad_score, hot_flat, preferred_element_type=jnp.float32)
    spread = spread.reshape(slot_count, local_heads, slot_len, 3, buckets)
    hot_exact = bucket_hot.astype(jnp.float32).reshape(slot_count, slot_len, 3, buckets)
    grad_table = jnp.einsum("cita,chitb->thab", hot_exact, spread, precision=highest)
    return (grad_weight, grad_table, grad_rows)


def local(
    tokens,
    spatial,
    box_coords,
    reading_order,
    page_len,
    w_attn,
    tables,
    w_out,
    ln_gain,
    ln_shift,
    w_up,
    w_down,
    grad_out,
):
    batches = tokens.shape[1]
    slot_count = page_len.shape[1]
    group_rows = box_coords.shape[3]
    slot_len = group_rows // slot_count
    buckets = tables.shape[4]
    coarse = COORD // buckets
    position = jnp.arange(slot_len, dtype=jnp.int32)
    weight_args = (w_attn, tables, w_out, ln_gain, ln_shift, w_up, w_down)
    totals = None
    results = []
    token_grads = []
    for batch_index in range(batches):
        gathered = fetch_weights(weight_args)
        attn_full, table_full, proj_own, proj_full, gain_full, shift_full, up_full, down_full = (
            gathered
        )
        own_rows = tokens[:, batch_index]
        rows_x, rows_s = (
            lax.all_gather(own_rows, "head", axis=1, tiled=True),
            lax.all_gather(spatial[:, batch_index], "head", axis=1, tiled=True),
        )
        page_id = position[None, :] // page_len[batch_index][:, None]
        same_page = page_id[:, :, None] == page_id[:, None, :]
        head_outs = []
        kept_states = []
        hot_sets = []
        for modality in range(2):
            bucket_ids = (
                reading_order[modality, batch_index],
                box_coords[modality, 0, batch_index] // coarse,
                box_coords[modality, 1, batch_index] // coarse,
            )
            bucket_hot = jnp.stack(
                [one_hot(index_row, buckets) for index_row in bucket_ids], axis=1
            )
            head_rows, kept_state = attend_forward(
                rows_x[modality],
                rows_s[modality],
                attn_full[modality],
                table_full[modality],
                bucket_hot,
                same_page,
            )
            head_outs.append(head_rows)
            kept_states.append(kept_state)
            hot_sets.append(bucket_hot)
        head_stack = jnp.stack(head_outs)
        exchanged = lax.all_to_all(head_stack, "head", split_axis=1, concat_axis=2, tiled=True)
        attn_sum = jnp.einsum(
            "srd,sde->re", exchanged, proj_full, preferred_element_type=jnp.float32
        )
        residual = own_rows[0].astype(jnp.float32) + own_rows[1].astype(jnp.float32) + attn_sum
        gain_rows = gain_full.astype(jnp.float32)
        shift_rows = shift_full.astype(jnp.float32)
        hidden, first_back = jax.vjp(layer_norm, residual, gain_rows[0], shift_rows[0])
        hidden_low = hidden.astype(jnp.bfloat16)
        hidden_all = lax.all_gather(hidden_low, "head", axis=0, tiled=True)
        pre_act = jnp.dot(hidden_all, up_full, preferred_element_type=jnp.float32)
        activated, gelu_back = jax.vjp(exact_gelu, pre_act)
        act_low = activated.astype(jnp.bfloat16)
        branch_part = jnp.dot(act_low, down_full, preferred_element_type=jnp.float32)
        branch = lax.psum_scatter(
            branch_part.astype(jnp.bfloat16), "head", scatter_dimension=0, tiled=True
        ).astype(jnp.float32)
        result, last_back = jax.vjp(layer_norm, hidden + branch, gain_rows[1], shift_rows[1])
        results.append(result.astype(jnp.bfloat16))
        grad_sum, grad_gain_two, grad_shift_two = last_back(
            grad_out[batch_index].astype(jnp.float32)
        )
        grad_branch = grad_sum.astype(jnp.bfloat16)
        grad_branch_all = lax.all_gather(grad_branch, "head", axis=0, tiled=True)
        grad_down = jnp.einsum(
            "rf,rd->fd", act_low, grad_branch_all, preferred_element_type=jnp.float32
        )
        grad_act = jnp.einsum(
            "rd,fd->rf", grad_branch_all, down_full, preferred_element_type=jnp.float32
        )
        grad_pre = gelu_back(grad_act)[0].astype(jnp.bfloat16)
        grad_up = jnp.einsum("rd,rf->df", hidden_all, grad_pre, preferred_element_type=jnp.float32)
        back_part = jnp.einsum("rf,df->rd", grad_pre, up_full, preferred_element_type=jnp.float32)
        back_part = lax.psum_scatter(
            back_part.astype(jnp.bfloat16), "head", scatter_dimension=0, tiled=True
        ).astype(jnp.float32)
        grad_hidden = grad_sum + back_part
        grad_res, grad_gain_one, grad_shift_one = first_back(grad_hidden)
        grad_attn = grad_res.astype(jnp.bfloat16)
        grad_attn_all = lax.all_gather(grad_attn, "head", axis=0, tiled=True)
        grad_proj = jnp.einsum(
            "srd,re->sde", head_stack, grad_attn_all, preferred_element_type=jnp.float32
        )
        grad_heads = jnp.einsum(
            "re,sde->srd", grad_attn_all, proj_own, preferred_element_type=jnp.float32
        ).astype(jnp.bfloat16)
        weight_parts = []
        table_parts = []
        row_parts = []
        for modality in range(2):
            grad_weight, grad_table, grad_rows = attend_backward(
                grad_heads[modality],
                kept_states[modality],
                rows_x[modality],
                rows_s[modality],
                attn_full[modality],
                hot_sets[modality],
                same_page,
            )
            weight_parts.append(grad_weight)
            table_parts.append(grad_table)
            row_parts.append(grad_rows)
        partial_rows = lax.psum_scatter(
            jnp.stack(row_parts).astype(jnp.bfloat16), "head", scatter_dimension=1, tiled=True
        ).astype(jnp.float32)
        token_grads.append((partial_rows + grad_res[None]).astype(jnp.bfloat16))
        step_grads = (
            jnp.stack(weight_parts),
            jnp.stack(table_parts),
            grad_proj,
            jnp.stack([grad_gain_one, grad_gain_two]),
            jnp.stack([grad_shift_one, grad_shift_two]),
            grad_up,
            grad_down,
        )
        totals = add_up(totals, reduce_grads(step_grads))
    return (jnp.stack(results), jnp.stack(token_grads, axis=1)) + totals


def solution(mesh):
    return jax.shard_map(
        local,
        mesh=mesh,
        in_specs=(
            P(None, None, ("page", "head"), None),
            P(None, None, ("page", "head"), None),
            P(None, None, None, "page"),
            P(None, None, "page"),
            P(None, "page"),
            P(None, None, "page", "head"),
            P(None, None, "head", "page", None),
            P(None, "head", "page"),
            P(None, ("page", "head")),
            P(None, ("page", "head")),
            P(None, ("page", "head")),
            P(("page", "head"), None),
            P(None, ("page", "head"), None),
        ),
        out_specs=(
            P(None, ("page", "head"), None),
            P(None, None, ("page", "head"), None),
            P(None, None, "page", "head"),
            P(None, None, "head", "page", None),
            P(None, "head", "page"),
            P(None, ("page", "head")),
            P(None, ("page", "head")),
            P(None, ("page", "head")),
            P(("page", "head"), None),
        ),
        check_vma=False,
    )
```

profile of v0, /device:TPU:0, one launch (start us, length us, event | category | flops | bytes accessed | tf_op | source)
XLA Modules:
  0.0 975.0 jit_solution(7931586554364305012)
XLA Ops:
  13.2 35.9 %all_gather.66 = bf16[2,192,768]{1,0,2:T(2,128)(2,1)S(1)} all-gather(bf16[2,192,96]{1,0,2:T(2,128)(2,1)S(1)} %copy.217), channel_id=1, replica_groups=mesh['page'=8,'head'=4] {'page'}, dimensions={2}, use_global_device_ids=true | all-gather | bytes 663552 | tf_op jit(solution)/shard_map/all_gather | solution.py:32
  52.6 35.2 %all_gather.65 = bf16[2,3,3,128,128]{4,3,1,2,0:T(8,128)(2,1)} all-gather(bf16[2,3,3,16,128]{4,3,1,2,0:T(8,128)(2,1)S(1)} %copy.209), channel_id=1, replica_groups=mesh['page'=8,'head'=4] {'page'}, dimensions={3}, use_global_device_ids=true | all-gather | bytes 663552 | tf_op jit(solution)/shard_map/all_gather | solution.py:31
  91.0 41.2 %all-gather.5 = bf16[32,24,2]{1,2,0:T(2,128)(2,1)S(1)} all-gather(bf16[1,24,2]{1,2,0:T(2,128)(2,1)S(1)} %bitcast.813), channel_id=1, replica_groups=mesh['page'=8,'head'=4] {'page','head'}, dimensions={0}, use_global_device_ids=true | all-gather | bytes 3168 | tf_op jit(solution)/shard_map/all_gather | solution.py:38
  133.1 36.4 %all-gather.4 = bf16[32,24,2]{1,2,0:T(2,128)(2,1)S(1)} all-gather(bf16[1,24,2]{1,2,0:T(2,128)(2,1)S(1)} %bitcast.814), channel_id=1, replica_groups=mesh['page'=8,'head'=4] {'page','head'}, dimensions={0}, use_global_device_ids=true | all-gather | bytes 3168 | tf_op jit(solution)/shard_map/all_gather | solution.py:37
  177.1 8.0 fusion.212
  185.1 6.5 copy.331
  194.9 3.5 fusion.211
  198.4 4.6 copy.332
  204.9 4.3 copy.329
  220.9 4.6 fusion.228
  233.3 5.3 fusion.231
  243.9 4.1 all-to-all-start
  261.3 6.8 fusion.235
  268.1 3.0 fusion.7
  275.7 7.0 fusion.238
  282.7 3.4 fusion.84
  293.0 9.7 all_gather.70
  302.6 7.2 multiply_convert_fusion.5
  309.8 3.2 convolution_convert_fusion.7
  313.1 2.6 fusion.85
  319.1 17.0 %all_to_all.36 = bf16[2,512,192]{2,0,1:T(2,128)(2,1)} all-to-all(bf16[2,512,192]{2,0,1:T(2,128)(2,1)} %copy.226), channel_id=1, replica_groups=mesh['page'=8,'head'=4] {'head'}, dimensions={1} | all-to-all | bytes 786432 | tf_op jit(solution)/shard_map/all_to_all | solution.py:227
  343.8 2.7 fusion.207
  346.5 7.4 all_gather.75
  353.9 5.5 multiply_convert_fusion.4
  365.5 17.3 %reduce-scatter.19.cloned.1.call-done = bf16[128,768]{1,0:T(8,128)(2,1)} async-done(((bf16[512,768]{1,0:T(8,128)(2,1)}), bf16[128,768]{1,0:T(8,128)(2,1)}) %reduce-scatter.19.cloned.1.call-update) | async-done | bytes 196624 | tf_op jit(solution)/shard_map/reduce_scatter | solution.py:241
  389.0 8.4 all_gather.76
  403.0 8.7 all_gather.78
  411.8 3.3 add_convert_fusion
  425.6 25.2 %reduce-scatter.25.cloned.1.call-done = bf16[128,768]{1,0:T(8,128)(2,1)} async-done(((bf16[512,768]{1,0:T(8,128)(2,1)}), bf16[128,768]{1,0:T(8,128)(2,1)}) %reduce-scatter.25.cloned.1.call-update) | async-done | bytes 196624 | tf_op jit(solution)/shard_map/reduce_scatter | solution.py:260
  455.0 8.2 all_gather.79
  464.6 9.3 all_gather.77
  494.7 3.4 copy.264
  501.7 3.5 copy.322
  505.2 3.2 reshape.1976
  508.5 2.8 fusion.120
  513.4 2.7 fusion.100
  522.8 2.8 fusion.124
  525.6 3.2 fusion.106
  558.3 2.9 maximum_add_fusion
  561.2 12.6 %copy.320 = f32[2,5,768,192]{3,1,0,2:T(8,128)} copy(f32[2,5,768,192]{2,3,1,0:T(8,128)} %maximum_add_fusion) | data formatting | bytes 11796480
  573.8 11.3 %reshape.1974 = f32[768,1920]{1,0:T(8,128)} reshape(f32[768,2,5,192]{3,2,1,0:T(8,128)} %bitcast.720) | data formatting | bytes 11796480
  598.6 39.9 %all-reduce.3 = (f32[2,768]{1,0:T(2,128)S(1)}, f32[2,768]{1,0:T(2,128)S(1)}) all-reduce(f32[2,768]{1,0:T(2,128)S(1)} %maximum_add_fusion.2, f32[2,768]{1,0:T(2,128)S(1)} %maximum_add_fusion.3), channel_id=22, replica_groups=mesh['page'=8,'head'=4] {'page','head'}, use_global_device_ids=true, to_apply=%region_42.44.clone | all-reduce | flops 3072 | bytes 24576
  641.4 4.5 reduce-scatter.35.cloned.1.call-done
  647.8 27.7 %reduce-scatter.27.cloned.1.call-done = bf16[2,128,768]{2,1,0:T(8,128)(2,1)} async-done(((bf16[2,512,768]{2,1,0:T(8,128)(2,1)}), bf16[2,128,768]{2,1,0:T(8,128)(2,1)}) %reduce-scatter.27.cloned.1.call-update) | async-done | bytes 393232 | tf_op jit(solution)/shard_map/reduce_scatter | solution.py:289
  676.7 29.5 %reduce-scatter.23.cloned.1.call-done = bf16[2,128,768]{2,1,0:T(8,128)(2,1)} async-done(((bf16[2,512,768]{2,1,0:T(8,128)(2,1)}), bf16[2,128,768]{2,1,0:T(8,128)(2,1)}) %reduce-scatter.23.cloned.1.call-update) | async-done | bytes 393232 | tf_op jit(solution)/shard_map/reduce_scatter | solution.py:289
  708.3 113.7 %reduce-scatter.33.cloned.1.call-done = f32[96,1920]{1,0:T(8,128)} async-done(((f32[768,1920]{1,0:T(8,128)}), f32[96,1920]{1,0:T(8,128)}) %reduce-scatter.33.cloned.1.call-update) | async-done | bytes 737296
  825.3 69.9 %reduce-scatter.29.cloned.1.call-done = f32[768,96]{0,1:T(8,128)} async-done(((f32[768,768]{0,1:T(8,128)}), f32[768,96]{0,1:T(8,128)}) %reduce-scatter.29.cloned.1.call-update) | async-done | bytes 294928 | tf_op jit(solution)/shard_map/reduce_scatter | solution.py:50
  895.3 72.7 %reduce-scatter.31.cloned.1.call-done = f32[96,768]{1,0:T(8,128)} async-done(((f32[768,768]{1,0:T(8,128)}), f32[96,768]{1,0:T(8,128)}) %reduce-scatter.31.cloned.1.call-update) | async-done | bytes 294928 | tf_op jit(solution)/shard_map/reduce_scatter | solution.py:51
  (689 shorter events, 204.1 us)
Async XLA Ops:
  7.2 169.9 %all-gather.15.cloned.1.call-start = ((), (), s32[]{:S(2)}) async-start(), calls=%async_computation.12 | async-start | bytes 4423680 | tf_op jit(solution)/shard_map/all_gather | solution.py:30
  9.7 182.0 %all-gather.23.cloned.1.call-start = ((), (), s32[]{:S(2)}) async-start(), calls=%async_computation.22 | async-start | bytes 1966080 | tf_op jit(solution)/shard_map/all_gather | solution.py:198
  10.8 192.3 %all-gather.25.cloned.1.call-start = ((), (), s32[]{:S(2)}) async-start(), calls=%async_computation.23 | async-start | bytes 1966080 | tf_op jit(solution)/shard_map/all_gather | solution.py:199
  11.8 236.7 %all-gather.27.cloned.1.call-start = ((), (), s32[]{:S(2)}) async-start(), calls=%async_computation.24 | async-start | bytes 1966080 | tf_op jit(solution)/shard_map/all_gather | solution.py:198
  12.4 239.0 %all-gather.29.cloned.1.call-start = ((), (), s32[]{:S(2)}) async-start(), calls=%async_computation.25 | async-start | bytes 1966080 | tf_op jit(solution)/shard_map/all_gather | solution.py:199
  13.0 276.6 %all-gather.17.cloned.1.call-start = ((), (), s32[]{:S(2)}) async-start(), calls=%async_computation.13 | async-start | bytes 2949120 | tf_op jit(solution)/shard_map/all_gather | solution.py:40
  13.1 39.2 %copy-start.177 = (s32[2,2,2,512]{3,2,1,0:T(2,128)S(1)}, s32[2,2,2,512]{3,2,1,0:T(2,128)}, u32[]{:S(2)}) copy-start(s32[2,2,2,512]{3,2,1,0:T(2,128)} %param.17) | copy-start | bytes 49156
  13.2 39.3 %copy-start.182 = (s32[2,2,512]{2,1,0:T(2,128)S(1)}, s32[2,2,512]{2,1,0:T(2,128)}, u32[]{:S(2)}) copy-start(s32[2,2,512]{2,1,0:T(2,128)} %param.18) | copy-start | bytes 24580
  13.2 39.4 %copy-start.158 = (bf16[2,3,3,16,128]{4,3,2,1,0:T(8,128)(2,1)S(1)}, bf16[2,3,3,16,128]{4,3,2,1,0:T(8,128)(2,1)}, u32[]{:S(2)}) copy-start(bf16[2,3,3,16,128]{4,3,2,1,0:T(8,128)(2,1)} %param.21) | copy-start | bytes 221188
  49.1 38.8 %copy-start.193 = (s32[2,1]{0,1:T(1,128)S(1)}, s32[2,1]{0,1:T(1,128)}, u32[]{:S(2)}) copy-start(s32[2,1]{0,1:T(1,128)} %param.19) | copy-start | bytes 28
  49.1 42.0 %copy-start.200 = (bf16[2,24]{1,0:T(2,128)(2,1)S(1)}, bf16[2,24]{1,0:T(2,128)(2,1)}, u32[]{:S(2)}) copy-start(bf16[2,24]{1,0:T(2,128)(2,1)} %param.24) | copy-start | bytes 292
  49.1 84.1 %copy-start.201 = (bf16[2,24]{1,0:T(2,128)(2,1)S(1)}, bf16[2,24]{1,0:T(2,128)(2,1)}, u32[]{:S(2)}) copy-start(bf16[2,24]{1,0:T(2,128)(2,1)} %param.23) | copy-start | bytes 292
  50.9 251.8 %all-gather.19.cloned.1.call-start = ((), (), s32[]{:S(2)}) async-start(), calls=%async_computation.14 | async-start | bytes 1327104 | tf_op jit(solution)/shard_map/all_gather | solution.py:33
  51.6 258.2 %all-gather.21.cloned.1.call-start = ((), (), s32[]{:S(2)}) async-start(), calls=%async_computation.15 | async-start | bytes 1327104 | tf_op jit(solution)/shard_map/all_gather | solution.py:34
  52.6 168.3 %copy-start.78 = (pred[512,1,128]{2,0,1:T(32,128)(4,1)}, pred[512,1,128]{2,0,1:T(32,128)(4,1)S(1)}, u32[]{:S(2)}) copy-start(pred[512,1,128]{2,0,1:T(32,128)(4,1)S(1)} %iota_compare_fusion.8) | copy-start | bytes 196612
  91.0 142.3 %copy-start.80 = (pred[512,1,128]{2,0,1:T(32,128)(4,1)}, pred[512,1,128]{2,0,1:T(32,128)(4,1)S(1)}, u32[]{:S(2)}) copy-start(pred[512,1,128]{2,0,1:T(32,128)(4,1)S(1)} %iota_compare_fusion.11) | copy-start | bytes 196612
  194.9 21.3 %copy-start.49 = (bf16[1,512,192]{1,2,0:T(8,128)(2,1)}, bf16[1,512,192]{1,2,0:T(8,128)(2,1)S(1)}, u32[]{:S(2)}) copy-start(bf16[1,512,192]{1,2,0:T(8,128)(2,1)S(1)} %get-tuple-element.106) | copy-start | bytes 589828
  194.9 21.3 %copy-start.51 = (bf16[1,512,192]{1,2,0:T(8,128)(2,1)}, bf16[1,512,192]{1,2,0:T(8,128)(2,1)S(1)}, u32[]{:S(2)}) copy-start(bf16[1,512,192]{1,2,0:T(8,128)(2,1)S(1)} %get-tuple-element.107) | copy-start | bytes 589828
  204.9 13.7 %copy-start.62 = (bf16[1,512,192]{1,2,0:T(8,128)(2,1)}, bf16[1,512,192]{1,2,0:T(8,128)(2,1)S(1)}, u32[]{:S(2)}) copy-start(bf16[1,512,192]{1,2,0:T(8,128)(2,1)S(1)} %get-tuple-element.126) | copy-start | bytes 589828
  204.9 13.7 %copy-start.64 = (bf16[1,512,192]{1,2,0:T(8,128)(2,1)}, bf16[1,512,192]{1,2,0:T(8,128)(2,1)S(1)}, u32[]{:S(2)}) copy-start(bf16[1,512,192]{1,2,0:T(8,128)(2,1)S(1)} %get-tuple-element.127) | copy-start | bytes 589828
  243.9 43.2 %all-to-all-start = ((bf16[2,512,192]{2,0,1:T(2,128)(2,1)}), bf16[2,512,192]{2,0,1:T(2,128)(2,1)}, u32[]{:S(2)}, u32[]{:S(2)}) async-start(bf16[2,512,192]{2,0,1:T(2,128)(2,1)} %copy.214), calls=%async_computation | async-start | bytes 1048576 | tf_op jit(solution)/shard_map/all_to_all | solution.py:227
  248.0 95.8 %reduce-scatter.17.cloned.1.call-start = ((), (), s32[]{:S(2)}) async-start(), calls=%async_computation.16 | async-start | bytes 983040 | tf_op jit(solution)/shard_map/reduce_scatter | solution.py:241
  313.0 69.8 %reduce-scatter.19.cloned.1.call-start = ((), (), s32[]{:S(2)}) async-start(), calls=%async_computation.17 | async-start | bytes 983040 | tf_op jit(solution)/shard_map/reduce_scatter | solution.py:241
  343.8 10.1 %copy-start.202 = (bf16[768,768]{0,1:T(8,128)(2,1)S(1)}, bf16[768,768]{0,1:T(8,128)(2,1)}, u32[]{:S(2)}) copy-start(bf16[768,768]{0,1:T(8,128)(2,1)} %all-gather.19.cloned.1.call-done) | copy-start | bytes 3538948
  361.9 63.7 %reduce-scatter.21.cloned.1.call-start = ((), (), s32[]{:S(2)}) async-start(), calls=%async_computation.18 | async-start | bytes 983040 | tf_op jit(solution)/shard_map/reduce_scatter | solution.py:260
  384.5 12.9 %copy-start.210 = (f32[512,768]{1,0:T(8,128)S(1)}, f32[512,768]{1,0:T(8,128)}, u32[]{:S(2)}) copy-start(f32[512,768]{1,0:T(8,128)} %get-tuple-element.158) | copy-start | bytes 4718596
  386.4 11.1 %copy-start.206 = (bf16[768,768]{1,0:T(8,128)(2,1)S(1)}, bf16[768,768]{1,0:T(8,128)(2,1)}, u32[]{:S(2)}) copy-start(bf16[768,768]{1,0:T(8,128)(2,1)} %all-gather.21.cloned.1.call-done) | copy-start | bytes 3538948
  386.4 11.1 %copy-start.209 = (f32[512,768]{1,0:T(8,128)S(1)}, f32[512,768]{1,0:T(8,128)}, u32[]{:S(2)}) copy-start(f32[512,768]{1,0:T(8,128)} %get-tuple-element.90) | copy-start | bytes 4718596
  388.2 9.3 copy-start.188
  401.2 49.6 %reduce-scatter.25.cloned.1.call-start = ((), (), s32[]{:S(2)}) async-start(), calls=%async_computation.20 | async-start | bytes 983040 | tf_op jit(solution)/shard_map/reduce_scatter | solution.py:260
  401.2 10.5 %copy-start.207 = (bf16[768,768]{1,0:T(8,128)(2,1)S(1)}, bf16[768,768]{1,0:T(8,128)(2,1)}, u32[]{:S(2)}) copy-start(bf16[768,768]{1,0:T(8,128)(2,1)} %all-gather.21.cloned.1.call-done) | copy-start | bytes 3538948
  401.9 9.8 %copy-start.190 = (f32[128]{0:T(128)}, f32[128]{0:T(128)S(1)}, u32[]{:S(2)}) copy-start(f32[128]{0:T(128)S(1)} %negate_multiply_fusion.3) | copy-start | bytes 1540
  417.7 222.1 %all-reduce.6.cloned.1.call-start = ((), (), s32[]{:S(2)}) async-start(), calls=%async_computation.30 | async-start | bytes 2359296
  417.9 7.7 copy-start.160
  454.1 9.1 copy-start.35
  463.7 20.1 %copy-start.46 = (bf16[1,512,192]{1,2,0:T(8,128)(2,1)}, bf16[1,512,192]{1,2,0:T(8,128)(2,1)S(1)}, u32[]{:S(2)}) copy-start(bf16[1,512,192]{1,2,0:T(8,128)(2,1)S(1)} %get-tuple-element.123) | copy-start | bytes 589828
  463.7 24.9 %copy-start.44 = (bf16[1,512,192]{1,2,0:T(8,128)(2,1)}, bf16[1,512,192]{1,2,0:T(8,128)(2,1)S(1)}, u32[]{:S(2)}) copy-start(bf16[1,512,192]{1,2,0:T(8,128)(2,1)S(1)} %get-tuple-element.122) | copy-start | bytes 589828
  464.6 10.1 %copy-start.1 = (f32[3,512,512]{1,2,0:T(8,128)S(1)}, f32[3,512,512]{1,2,0:T(8,128)}, u32[]{:S(2)}) copy-start(f32[3,512,512]{1,2,0:T(8,128)} %copy-done) | copy-start | bytes 9437188
  464.6 10.1 %copy-start.118 = (bf16[1,512,192]{1,2,0:T(8,128)(2,1)S(1)}, bf16[1,512,192]{1,2,0:T(8,128)(2,1)}, u32[]{:S(2)}) copy-start(bf16[1,512,192]{1,2,0:T(8,128)(2,1)} %get-tuple-element.108) | copy-start | bytes 589828
  464.6 10.1 %copy-start.153 = (f32[3,512]{1,0:T(4,128)S(1)}, f32[3,512]{1,0:T(4,128)}, u32[]{:S(2)}) copy-start(f32[3,512]{1,0:T(4,128)} %log_add_fusion.2) | copy-start | bytes 18436
  498.1 147.8 %reduce-scatter.35.cloned.1.call-start = ((), (), s32[]{:S(2)}) async-start(), calls=%async_computation.29 | async-start | bytes 1327104
  511.3 164.3 %reduce-scatter.27.cloned.1.call-start = ((), (), s32[]{:S(2)}) async-start(), calls=%async_computation.21 | async-start | bytes 1966080 | tf_op jit(solution)/shard_map/reduce_scatter | solution.py:289
  528.8 177.4 %reduce-scatter.23.cloned.1.call-start = ((), (), s32[]{:S(2)}) async-start(), calls=%async_computation.19 | async-start | bytes 1966080 | tf_op jit(solution)/shard_map/reduce_scatter | solution.py:289
  547.0 275.0 %reduce-scatter.33.cloned.1.call-start = ((), (), s32[]{:S(2)}) async-start(), calls=%async_computation.28 | async-start | bytes 6635520
  585.2 310.1 %reduce-scatter.29.cloned.1.call-start = ((), (), s32[]{:S(2)}) async-start(), calls=%async_computation.26 | async-start | bytes 2654208 | tf_op jit(solution)/shard_map/reduce_scatter | solution.py:50
  590.7 377.3 %reduce-scatter.31.cloned.1.call-start = ((), (), s32[]{:S(2)}) async-start(), calls=%async_computation.27 | async-start | bytes 2654208 | tf_op jit(solution)/shard_map/reduce_scatter | solution.py:51
  595.4 80.2 %copy-start.103 = (f32[128,768]{1,0:T(8,128)S(1)}, f32[128,768]{1,0:T(8,128)}, u32[]{:S(2)}) copy-start(f32[128,768]{1,0:T(8,128)} %get-tuple-element.82) | copy-start | bytes 1179652
  597.7 108.5 %copy-start.104 = (f32[128,768]{1,0:T(8,128)S(1)}, f32[128,768]{1,0:T(8,128)}, u32[]{:S(2)}) copy-start(f32[128,768]{1,0:T(8,128)} %get-tuple-element.76) | copy-start | bytes 1179652
  (183 other events, 406.6 us)
Sparse Core Ops, SparseCore 0:
  10.8 88.0 all-gather.14
  101.0 18.4 all-gather.22
  121.1 19.6 all-gather.24
  142.3 19.7 all-gather.26
  163.4 19.6 all-gather.28
  184.5 24.0 all-gather.16
  210.8 41.0 all-gather.18
  254.1 39.9 all-gather.20
  313.1 24.0 reduce-scatter.16
  362.1 20.7 reduce-scatter.18
  401.3 23.6 reduce-scatter.20
  427.6 23.2 reduce-scatter.24
  498.3 80.4 all-reduce.5
  582.4 63.5 reduce-scatter.34
  648.5 27.0 reduce-scatter.26
  678.0 28.1 reduce-scatter.22
  710.2 111.7 reduce-scatter.32
  826.3 68.8 reduce-scatter.28
  899.7 68.1 reduce-scatter.30
where the time goes:
time: 985 us; the launch traced here: 975 us
  waiting for transfers between devices  363 us (37%)
  blocking collectives  257 us (26%)
  matrix products  152 us (15%)
  local copies, waits for them, and re-layouts  125 us (13%)
  other arithmetic  52.5 us (5%)
  between operations  18.9 us (2%)
    unnamed x22, waiting for transfers between devices  121 us
    unnamed x443, local copies, waits for them, and re-layouts  85.3 us
    reduce_scatter x1, waiting for transfers between devices, reduce_grads(): lax.psum_scatter(grad_down, 'page', scatter_dimension=0, tiled=True)  72.7 us
    reduce_scatter x1, waiting for transfers between devices, reduce_grads(): lax.psum_scatter(grad_up, 'page', scatter_dimension=1, tiled=True)  69.9 us
    reduce_scatter x2, waiting for transfers between devices, local(): lax.psum_scatter(jnp.stack(row_parts).astype(jnp.bfloat16), 'head', scatt...  57.3 us
    all_gather x1, blocking collectives, fetch_weights(): lax.all_gather(ln_shift, ('page', 'head'), axis=1, tiled=True)  41.2 us
    unnamed x1, blocking collectives  39.9 us
    all_gather x1, blocking collectives, fetch_weights(): lax.all_gather(ln_gain, ('page', 'head'), axis=1, tiled=True)  36.4 us
  transfers between devices with their start and end apart: 20, of which 8 were waited for; matrix products, arithmetic and copies ran while one was open for 26% of the time, Pallas kernels for 0%

commit v1 on v0

v1 whole, which is shorter than its diff:
```python
import functools

import jax
import jax.numpy as jnp
from jax import lax
from jax.experimental import pallas as pl
from jax.experimental.pallas import tpu as pltpu
from jax.sharding import PartitionSpec as P

COORD = 1024
f32 = jnp.float32
bf16 = jnp.bfloat16


def layer_norm(value, gain, shift):
    center = jnp.mean(value, axis=-1, keepdims=True)
    centred = value - center
    variance = jnp.mean(centred * centred, axis=-1, keepdims=True)
    return centred * lax.rsqrt(variance + 1e-05) * gain + shift


def swap(value, axis, mask):
    count = lax.axis_size(axis)
    return lax.ppermute(value, axis, [(place, place ^ mask) for place in range(count)])


def gather_rows(own):
    two = jnp.stack([own, swap(own, "head", 2)])
    four = jnp.concatenate([two, swap(two, "head", 1)])
    return four.reshape((4 * own.shape[0],) + own.shape[1:])


def scatter_rows(part):
    blocks = part.reshape((4, part.shape[0] // 4) + part.shape[1:])
    half = blocks[:2].astype(f32) + swap(blocks[2:].astype(bf16), "head", 1).astype(f32)
    return half[0] + swap(half[1].astype(bf16), "head", 2).astype(f32)


def page_bits():
    count = lax.axis_size("page")
    return [1 << bit for bit in reversed(range(count.bit_length() - 1))]


def gather_pages(own):
    full = own
    for depth, mask in enumerate(page_bits()):
        full = jnp.stack([full, swap(full, "page", mask)], axis=depth)
    return full.reshape((lax.axis_size("page"),) + own.shape)


def scatter_pages(blocks):
    masks = page_bits()
    part = blocks.reshape((2,) * len(masks) + blocks.shape[1:])
    for depth in reversed(range(len(masks))):
        keep = lax.index_in_dim(part, 0, depth, keepdims=False)
        send = lax.index_in_dim(part, 1, depth, keepdims=False).astype(bf16)
        part = keep.astype(f32) + swap(send, "page", masks[depth]).astype(f32)
    return part


def by_page(blocks):
    count = blocks.shape[0]
    order = jnp.arange(count, dtype=jnp.int32) ^ lax.axis_index("page")
    return jnp.take(blocks, order, axis=0)


def dot(left, right, dims):
    return lax.dot_general(left, right, (dims, ((), ())), preferred_element_type=f32)


AB = ((1,), (0,))
ABT = ((1,), (1,))
ATB = ((0,), (0,))


def hot_columns(ids_ref, which, buckets):
    rows = ids_ref.shape[0]
    lane = lax.broadcasted_iota(jnp.int32, (rows, buckets), 1)
    return jnp.where(ids_ref[:, which : which + 1] == lane, 1.0, 0.0).astype(bf16)


def attend_kernel(x_ref, s_ref, w_ref, table_ref, out_ref, idc_ref, idr_ref, proj_ref, prob_ref, head_ref, part_ref):
    heads, buckets = table_ref.shape[0], table_ref.shape[1]
    width = heads * 64
    proj_ref[:, : 3 * width] = dot(x_ref[...], w_ref[:, : 3 * width], AB).astype(bf16)
    proj_ref[:, 3 * width :] = dot(s_ref[...], w_ref[:, 3 * width :], AB).astype(bf16)
    hots = [hot_columns(idc_ref, which, buckets) for which in range(3)]
    same = idc_ref[:, 3:4] == idr_ref[3:4, :]
    for head in range(heads):
        at = [slice(which * width + head * 64, which * width + head * 64 + 64) for which in range(5)]
        tabled = [
            dot(hots[which], table_ref[head, :, which * buckets : (which + 1) * buckets], AB).astype(bf16)
            for which in range(3)
        ]
        left = jnp.concatenate(
            [proj_ref[:, at[0]] * bf16(0.125), proj_ref[:, at[3]] * bf16(0.125)] + tabled, axis=1
        )
        right = jnp.concatenate([proj_ref[:, at[1]], proj_ref[:, at[4]]] + hots, axis=1)
        score = jnp.where(same, dot(left, right, ABT), -1e30)
        top = jnp.max(score, axis=1, keepdims=True)
        weight = jnp.exp(score - top)
        total = jnp.sum(weight, axis=1, keepdims=True)
        prob = (weight / total).astype(bf16)
        prob_ref[head] = prob
        head_ref[:, head * 64 : head * 64 + 64] = dot(prob, proj_ref[:, at[2]], AB).astype(bf16)
    part_ref[...] = dot(head_ref[...], out_ref[...], ABT)


def attend(rows_x, rows_s, weight, table, out_t, ids_col, ids_row):
    rows, heads = rows_x.shape[0], table.shape[0]
    return pl.pallas_call(
        attend_kernel,
        out_shape=(
            jax.ShapeDtypeStruct((rows, weight.shape[1]), bf16),
            jax.ShapeDtypeStruct((heads, rows, rows), bf16),
            jax.ShapeDtypeStruct((rows, heads * 64), bf16),
            jax.ShapeDtypeStruct((rows, out_t.shape[0]), f32),
        ),
        compiler_params=pltpu.CompilerParams(vmem_limit_bytes=48 * 1024 * 1024),
        name="attend",
    )(rows_x, rows_s, weight, table, out_t, ids_col, ids_row)


def attend_back_kernel(grad_ref, proj_ref, prob_ref, w_ref, out_ref, idc_ref, idr_ref, dproj_ref, dtable_ref, rows_ref):
    heads, rows = prob_ref.shape[0], prob_ref.shape[1]
    buckets = dtable_ref.shape[1]
    width = heads * 64
    grad_heads = dot(grad_ref[...], out_ref[...], AB).astype(bf16)
    hots = [hot_columns(idc_ref, which, buckets) for which in range(3)]
    bucket = lax.broadcasted_iota(jnp.int32, (buckets, rows), 0)
    hots_t = [
        jnp.where(idr_ref[which : which + 1, :] == bucket, 1.0, 0.0).astype(bf16) for which in range(3)
    ]
    for head in range(heads):
        at = [slice(which * width + head * 64, which * width + head * 64 + 64) for which in range(5)]
        prob = prob_ref[head]
        grad_out = grad_heads[:, head * 64 : head * 64 + 64]
        grad_prob = dot(grad_out, proj_ref[:, at[2]], ABT)
        weighted = prob.astype(f32) * grad_prob
        row_dot = jnp.sum(weighted, axis=1, keepdims=True)
        grad_score = (weighted - prob.astype(f32) * row_dot).astype(bf16)
        dproj_ref[:, at[2]] = dot(prob, grad_out, ATB).astype(bf16)
        right = jnp.concatenate([proj_ref[:, at[1]], proj_ref[:, at[4]]] + hots, axis=1)
        spread = dot(grad_score, right, AB)
        dproj_ref[:, at[0]] = (spread[:, :64] * 0.125).astype(bf16)
        dproj_ref[:, at[3]] = (spread[:, 64:128] * 0.125).astype(bf16)
        left = jnp.concatenate([proj_ref[:, at[0]], proj_ref[:, at[3]]], axis=1)
        grad_keys = dot(grad_score, left, ATB) * 0.125
        dproj_ref[:, at[1]] = grad_keys[:, :64].astype(bf16)
        dproj_ref[:, at[4]] = grad_keys[:, 64:].astype(bf16)
        for which in range(3):
            piece = spread[:, 128 + which * buckets : 128 + (which + 1) * buckets].astype(bf16)
            dtable_ref[head, :, which * buckets : (which + 1) * buckets] = dot(hots_t[which], piece, AB)
    rows_ref[...] = dot(dproj_ref[:, : 3 * width], w_ref[:, : 3 * width], ABT)


def attend_back(grad_all, proj, prob, weight, out_t, ids_col, ids_row, buckets):
    rows, heads = proj.shape[0], prob.shape[0]
    return pl.pallas_call(
        attend_back_kernel,
        out_shape=(
            jax.ShapeDtypeStruct(proj.shape, bf16),
            jax.ShapeDtypeStruct((heads, buckets, 3 * buckets), f32),
            jax.ShapeDtypeStruct((rows, weight.shape[0]), f32),
        ),
        compiler_params=pltpu.CompilerParams(vmem_limit_bytes=48 * 1024 * 1024),
        name="attend_back",
    )(grad_all, proj, prob, weight, out_t, ids_col, ids_row)


def local(
    tokens,
    spatial,
    box_coords,
    reading_order,
    page_len,
    w_attn,
    tables,
    w_out,
    ln_gain,
    ln_shift,
    w_up,
    w_down,
    grad_out,
):
    batches, own_count = tokens.shape[1], tokens.shape[2]
    features = tokens.shape[3]
    rows = box_coords.shape[3]
    buckets = tables.shape[4]
    heads = tables.shape[2]
    own_width = w_attn.shape[3]
    share = w_attn.shape[2]
    coarse = COORD // buckets
    head_index = lax.axis_index("head")
    modality = head_index // 2
    pages = lax.axis_size("page")

    def mine(value):
        return lax.dynamic_index_in_dim(value, modality, 0, keepdims=False)

    def other(value):
        return lax.dynamic_index_in_dim(value, 1 - modality, 0, keepdims=False)

    def bundle_attn(pick):
        attn = pick(w_attn).transpose(1, 0, 2)
        table = pick(tables)
        proj = pick(w_out).T
        return attn, table, proj

    attn_own, table_own, proj_own = bundle_attn(mine)
    attn_send, table_send, proj_send = bundle_attn(other)
    attn_got = swap(attn_send, "head", 2)
    table_got = swap(table_send, "head", 2)
    proj_got = swap(proj_send, "head", 2)
    attn_share = jnp.stack([attn_own, attn_got], axis=2).reshape(share, -1)
    table_share = jnp.concatenate([table_own, table_got], axis=1).transpose(1, 2, 0, 3)
    table_share = table_share.reshape(share, 3 * buckets)
    proj_share = jnp.concatenate([proj_own, proj_got], axis=1)
    bundle = jnp.concatenate([attn_share, proj_share, table_share], axis=1)
    bundle_full = by_page(gather_pages(bundle))
    attn_cols = 10 * own_width
    proj_cols = 2 * own_width
    weight = bundle_full[..., :attn_cols].reshape(features, attn_cols)
    out_t = bundle_full[..., attn_cols : attn_cols + proj_cols].reshape(features, proj_cols)
    table = bundle_full[..., attn_cols + proj_cols :]
    table = table.reshape(pages, 2 * heads, buckets // pages, 3 * buckets).transpose(1, 0, 2, 3)
    table = table.reshape(2 * heads, buckets, 3 * buckets)

    keep_rows = jnp.stack([mine(tokens), mine(spatial)])
    send_rows = jnp.stack([other(tokens), other(spatial)])
    two = jnp.stack([keep_rows, swap(send_rows, "head", 2)], axis=2)
    four = jnp.concatenate([two, swap(two, "head", 1)], axis=2)
    rows_full = four.reshape(2, batches, rows, features)

    ff_full = gather_pages(jnp.concatenate([w_up.T, w_down], axis=1))
    up_t = ff_full[..., :features].reshape(-1, features)
    down = ff_full[..., features:].reshape(-1, features)

    norms = jnp.stack([ln_gain, ln_shift])
    order = jnp.array([0, 2, 1, 3], jnp.int32)
    norms_head = gather_rows(norms[None])
    slots = jnp.take(order, jnp.arange(4, dtype=jnp.int32) ^ head_index)
    norms_head = jnp.take(norms_head, slots, axis=0)
    norms_full = by_page(gather_pages(norms_head))
    norms_full = norms_full.transpose(2, 3, 0, 1, 4).reshape(2, 2, features).astype(f32)
    gain, shift = norms_full[0], norms_full[1]

    blocks = order ^ head_index
    ids = jnp.concatenate(
        [
            mine(reading_order)[None],
            mine(box_coords) // coarse,
        ]
    )
    ids = jnp.concatenate(
        [ids, jnp.arange(rows, dtype=jnp.int32)[None, None] // page_len.reshape(1, batches, 1)]
    )
    ids = jnp.take(ids.reshape(4, batches, 4, own_count), blocks, axis=2).reshape(4, batches, rows)

    saved = []
    for batch in range(batches):
        ids_row = ids[:, batch]
        ids_col = ids_row.T
        proj, prob, head_rows, part = attend(
            rows_full[0, batch], rows_full[1, batch], weight, table, out_t, ids_col, ids_row
        )
        saved.append((ids_row, ids_col, proj, prob, head_rows, part))

    results, token_grads, dprojs = [], [], []
    dtable = dout = dgain = dshift = dup = ddown = 0.0
    for batch in range(batches):
        ids_row, ids_col, proj, prob, head_rows, part = saved[batch]
        attn_sum = scatter_rows(part)
        residual = tokens[0, batch].astype(f32) + tokens[1, batch].astype(f32) + attn_sum
        hidden, first_back = jax.vjp(layer_norm, residual, gain[0], shift[0])
        hidden_all = gather_rows(hidden.astype(bf16))
        pre_act = dot(hidden_all, up_t, ABT)
        cdf = 0.5 * (1.0 + lax.erf(pre_act * 0.7071067811865476))
        act = (pre_act * cdf).astype(bf16)
        slope = cdf + pre_act * jnp.exp(-0.5 * pre_act * pre_act) * 0.3989422804014327
        branch = scatter_rows(dot(act, down, AB))
        result, last_back = jax.vjp(layer_norm, hidden + branch, gain[1], shift[1])
        results.append(result.astype(bf16))
        grad_sum, gain_two, shift_two = last_back(grad_out[batch].astype(f32))
        branch_all = gather_rows(grad_sum.astype(bf16))
        ddown = ddown + dot(act, branch_all, ATB)
        grad_pre = (dot(branch_all, down, ABT) * slope).astype(bf16)
        dup = dup + dot(grad_pre, hidden_all, ATB)
        grad_hidden = grad_sum + scatter_rows(dot(grad_pre, up_t, AB))
        grad_res, gain_one, shift_one = first_back(grad_hidden)
        dgain = dgain + jnp.stack([gain_one, gain_two])
        dshift = dshift + jnp.stack([shift_one, shift_two])
        grad_all = gather_rows(grad_res.astype(bf16))
        dout = dout + dot(grad_all, head_rows, ATB)
        dproj, dtable_part, grad_rows = attend_back(
            grad_all, proj, prob, weight, out_t, ids_col, ids_row, buckets
        )
        dtable = dtable + dtable_part
        dprojs.append(dproj)
        row_blocks = grad_rows.reshape(4, own_count, features)
        half = row_blocks[:2] + swap(row_blocks[2:].astype(bf16), "head", 1).astype(f32)
        from_other = swap(half[1].astype(bf16), "head", 2).astype(f32)
        both = jnp.where(modality == 0, jnp.stack([half[0], from_other]), jnp.stack([from_other, half[0]]))
        token_grads.append((both + grad_res[None]).astype(bf16))

    dprojs = jnp.concatenate(dprojs)
    all_x = rows_full[0].reshape(-1, features)
    all_s = rows_full[1].reshape(-1, features)
    split = 6 * own_width
    dweight = jnp.concatenate(
        [dot(all_x, dprojs[:, :split], ATB), dot(all_s, dprojs[:, split:], ATB)], axis=1
    ).astype(bf16)

    dff = jnp.concatenate([dup.astype(bf16), ddown.astype(bf16)], axis=1)
    dff = scatter_pages(dff.reshape(pages, -1, 2 * features))
    dup_share = dff[:, :features].T
    ddown_share = dff[:, features:]

    dnorms = jnp.stack([dgain, dshift]).reshape(2, 2, pages, 4, -1).transpose(3, 2, 0, 1, 4)
    dnorms = jnp.take(dnorms, blocks, axis=0)
    half = dnorms[:2] + swap(dnorms[2:], "head", 1)
    dnorms = half[0] + swap(half[1], "head", 2)
    dnorms = scatter_pages(by_page(dnorms))

    dtable = dtable.reshape(2 * heads, pages, buckets // pages, 3 * buckets).transpose(1, 0, 2, 3)
    dtable = dtable.reshape(pages, share, 3 * buckets).astype(bf16)
    dbundle = jnp.concatenate(
        [dweight.reshape(pages, share, attn_cols), dout.astype(bf16).reshape(pages, share, proj_cols), dtable],
        axis=2,
    )
    dbundle = scatter_pages(by_page(dbundle))
    dattn = dbundle[:, :attn_cols].reshape(share, 5, 2, own_width).transpose(2, 1, 0, 3)
    dproj_out = dbundle[:, attn_cols : attn_cols + proj_cols].reshape(share, 2, own_width).transpose(1, 2, 0)
    dtable = dbundle[:, attn_cols + proj_cols :].reshape(2, heads, buckets // pages, 3, buckets)
    dtable = dtable.transpose(0, 3, 1, 2, 4)

    def both_modalities(pair):
        got = swap(pair[1].astype(bf16), "head", 2).astype(f32)
        return jnp.where(modality == 0, jnp.stack([pair[0], got]), jnp.stack([got, pair[0]]))

    return (
        jnp.stack(results),
        jnp.stack(token_grads, axis=1),
        both_modalities(dattn),
        both_modalities(dtable),
        both_modalities(dproj_out),
        dnorms[0],
        dnorms[1],
        dup_share,
        ddown_share,
    )


def solution(mesh):
    return jax.shard_map(
        local,
        mesh=mesh,
        in_specs=(
            P(None, None, ("page", "head"), None),
            P(None, None, ("page", "head"), None),
            P(None, None, None, "page"),
            P(None, None, "page"),
            P(None, "page"),
            P(None, None, "page", "head"),
            P(None, None, "head", "page", None),
            P(None, "head", "page"),
            P(None, ("page", "head")),
            P(None, ("page", "head")),
            P(None, ("page", "head")),
            P(("page", "head"), None),
            P(None, ("page", "head"), None),
        ),
        out_specs=(
            P(None, ("page", "head"), None),
            P(None, None, ("page", "head"), None),
            P(None, None, "page", "head"),
            P(None, None, "head", "page", None),
            P(None, "head", "page"),
            P(None, ("page", "head")),
            P(None, ("page", "head")),
            P(None, ("page", "head")),
            P(("page", "head"), None),
        ),
        check_vma=False,
    )
```

time: 985 us -> 498 us (0.51)
  blocking collectives: 257 us -> 0 us
  matrix products: 152 us -> 17.5 us
  waiting for transfers between devices: 363 us -> 244 us
  local copies, waits for them, and re-layouts: 125 us -> 69.3 us
  starting transfers between devices: 5.78 us -> 61.3 us
  Pallas kernels: 0 us -> 46.3 us
  between operations: 18.9 us -> 2.8 us
    ppermute x0 -> x58, waiting for transfers between devices: none -> 244 us  [swap(): lax.ppermute(value, axis, [(place, place ^ mask) for place in range(count)])]
    reduce_scatter x8 -> x0, waiting for transfers between devices: 243 us -> none  [the longest x1 72.7 us: reduce_grads(): lax.psum_scatter(grad_down, 'page', scatter_dimension=0, tiled=True)]
    all_gather x10 -> x0, blocking collectives: 200 us -> none  [the longest x1 41.2 us: fetch_weights(): lax.all_gather(ln_shift, ('page', 'head'), axis=1, tiled=True)]
    dot_general x86 -> x16, matrix products: 152 us -> 17.5 us  [dot(): lax.dot_general(left, right, (dims, ((), ())), preferred_element_type=f32)]
    unnamed x22 -> x0, waiting for transfers between devices: 121 us -> none
    unnamed x443 -> x140, local copies, waits for them, and re-layouts: 85.3 us -> 14.8 us
    ppermute x0 -> x58, starting transfers between devices: none -> 61.3 us  [swap(): lax.ppermute(value, axis, [(place, place ^ mask) for place in range(count)])]
    pallas_call x0 -> x4, Pallas kernels: none -> 46.3 us  [the longest x2 24.3 us: attend_back(): pl.pallas_call(attend_back_kernel, out_shape=(jax.ShapeDtypeStruct(proj.s...]
  transfers between devices with their start and end apart: 20 -> 58, of which waited for: 8 -> 28; matrix products, arithmetic and copies ran while one was open for 26% -> 21% of each run, Pallas kernels for 0% -> 9%
where the time goes in v1:
time: 498 us; the launch traced here: 494 us
  waiting for transfers between devices  244 us (49%)
  local copies, waits for them, and re-layouts  69.3 us (14%)
  starting transfers between devices  61.3 us (12%)
  other arithmetic  51.8 us (10%)
  Pallas kernels  46.3 us (9%)
  matrix products  17.5 us (4%)
    ppermute x58, waiting for transfers between devices, swap(): lax.ppermute(value, axis, [(place, place ^ mask) for place in range(count)])  244 us
    ppermute x58, starting transfers between devices, swap(): lax.ppermute(value, axis, [(place, place ^ mask) for place in range(count)])  61.3 us
    pallas_call x2, Pallas kernels, attend_back(): pl.pallas_call(attend_back_kernel, out_shape=(jax.ShapeDtypeStruct(proj.s...  24.3 us
    pallas_call x2, Pallas kernels, attend(): pl.pallas_call(attend_kernel, out_shape=(jax.ShapeDtypeStruct((rows, weig...  22 us
    dot_general x16, matrix products, dot(): lax.dot_general(left, right, (dims, ((), ())), preferred_element_type=f32)  17.5 us
    unnamed x140, local copies, waits for them, and re-layouts  14.8 us
    gather x5, local copies, waits for them, and re-layouts, by_page(): return jnp.take(blocks, order, axis=0)  12.3 us
  transfers between devices with their start and end apart: 58, of which 28 were waited for; matrix products, arithmetic and copies ran while one was open for 21% of the time, Pallas kernels for 9%

profile of v1, /device:TPU:0, one launch (start us, length us, event | category | flops | bytes accessed | tf_op | source)
XLA Modules:
  0.0 493.5 jit_solution(2574271286673195416)
XLA Ops:
  1.5 3.0 collective-permute-start.10
  6.3 2.1 collective-permute-start.3
  10.4 3.1 collective-permute-start.17
  19.3 2.5 collective-permute-start.5
  21.8 26.2 %collective-permute-done.5 = bf16[96,2688]{1,0:T(8,128)(2,1)S(1)} collective-permute-done((bf16[96,2688]{1,0:T(8,128)(2,1)S(1)}, bf16[96,2688]{1,0:T(8,128)(2,1)S(1)}, u32[]{:S(2)}, u32[]{:S(2)}) %collective-permute-start.5) | collective-permute-done | bytes 516128 | tf_op jit(solution)/shard_map/ppermute | solution.py:24
  51.9 21.3 %collective-permute-done.6 = bf16[2,96,2688]{2,1,0:T(8,128)(2,1)} collective-permute-done((bf16[2,96,2688]{2,1,0:T(8,128)(2,1)}, bf16[2,96,2688]{2,1,0:T(8,128)(2,1)}, u32[]{:S(2)}, u32[]{:S(2)}) %collective-permute-start.6) | collective-permute-done | bytes 1032224 | tf_op jit(solution)/shard_map/ppermute | solution.py:24
  73.1 3.4 fusion.80
  80.6 3.4 collective-permute-start.12
  87.5 1.9 collective-permute-done.13
  90.0 32.4 %collective-permute-done.14 = bf16[2,2,4,2,2,24]{5,4,3,2,0,1:T(2,128)(2,1)S(1)} collective-permute-done((bf16[2,2,4,2,2,24]{5,4,3,2,0,1:T(2,128)(2,1)S(1)}, bf16[2,2,4,2,2,24]{5,4,3,2,0,1:T(2,128)(2,1)S(1)}, u32[]{:S(2)}, u32[]{:S(2)}) %collective-permute-start.14) | collective-permute-done | bytes 3104 | tf_op jit(solution)/shard_map/ppermute | solution.py:24
  128.5 2.0 pad_maximum_fusion
  130.4 2.3 copy.113
  132.8 5.1 %gather_fusion.6 = bf16[8,96,2688]{2,1,0:T(8,128)(2,1)} fusion(bf16[8,96,2688]{2,1,0:T(8,128)(2,1)} %bitcast.434, s32[1024]{0:T(1024)S(1)} %get-tuple-element.172), kind=kCustom, calls=%fused_computation.clone | custom fusion | bytes 8257568 | tf_op jit(solution)/shard_map/jit(_take)/gather | solution.py:64
  137.9 2.6 broadcast_select_fusion.1
  143.7 10.7 %attend.2 = (bf16[512,1920]{1,0:T(8,128)(2,1)}, bf16[6,512,512]{2,1,0:T(8,128)(2,1)}, bf16[512,384]{1,0:T(8,128)(2,1)S(1)}, f32[512,768]{1,0:T(8,128)S(1)}) custom-call(bf16[512,768]{1,0:T(8,128)(2,1)S(1)} %copy-done.2, bf16[512,768]{1,0:T(8,128)(2,1)S(1)} %get-tuple-element.113.s_ref, bf16[768,1920]{1,0:T(8,128)(2,1)} %bitcast.428, ...), custom_call_target="tpu_custom_call" | custom-call | tf_op jit(solution)/shard_map/attend/pallas_call | solution.py:111
  157.9 2.5 collective-permute-start.18
  160.5 11.3 %attend.3 = (bf16[512,1920]{1,0:T(8,128)(2,1)}, bf16[6,512,512]{2,1,0:T(8,128)(2,1)}, bf16[512,384]{1,0:T(8,128)(2,1)S(1)}, f32[512,768]{1,0:T(8,128)S(1)}) custom-call(bf16[512,768]{1,0:T(8,128)(2,1)S(1)} %get-tuple-element.115.x_ref, bf16[512,768]{1,0:T(8,128)(2,1)S(1)} %get-tuple-element.114.s_ref, bf16[768,1920]{1,0:T(8,128)(2,1)} %bitcast.429, ...), custom_call_target="tpu_custom_call" | custom-call | tf_op jit(solution)/shard_map/attend/pallas_call | solution.py:111
  177.3 3.8 collective-permute-done.9
  181.1 3.6 collective-permute-done.23
  187.0 4.6 collective-permute-done.15
  191.8 11.6 %collective-permute-done.19 = bf16[2,2,96,1536]{3,2,1,0:T(8,128)(2,1)S(1)} collective-permute-done((bf16[2,2,96,1536]{3,2,1,0:T(8,128)(2,1)S(1)}, bf16[2,2,96,1536]{3,2,1,0:T(8,128)(2,1)S(1)}, u32[]{:S(2)}, u32[]{:S(2)}) %collective-permute-start.19) | collective-permute-done | bytes 1179680 | tf_op jit(solution)/shard_map/ppermute | solution.py:24
  203.9 2.0 multiply_convert_fusion.1
  210.4 5.4 %collective-permute-done.21 = bf16[128,768]{1,0:T(8,128)(2,1)S(1)} collective-permute-done((bf16[128,768]{1,0:T(8,128)(2,1)S(1)}, bf16[128,768]{1,0:T(8,128)(2,1)S(1)}, u32[]{:S(2)}, u32[]{:S(2)}) %collective-permute-start.21) | collective-permute-done | bytes 196640 | tf_op jit(solution)/shard_map/ppermute | solution.py:24
  217.6 4.6 collective-permute-done.24
  226.2 2.0 multiply_convert_fusion
  231.0 2.1 fusion.99
  233.1 2.6 copy.129
  235.7 2.6 copy.130
  242.1 5.5 %collective-permute-done.27 = bf16[128,768]{1,0:T(8,128)(2,1)S(1)} collective-permute-done((bf16[128,768]{1,0:T(8,128)(2,1)S(1)}, bf16[128,768]{1,0:T(8,128)(2,1)S(1)}, u32[]{:S(2)}, u32[]{:S(2)}) %collective-permute-start.27) | collective-permute-done | bytes 196640 | tf_op jit(solution)/shard_map/ppermute | solution.py:24
  251.4 3.9 collective-permute-done.36
  258.7 5.9 %collective-permute-done.28 = bf16[128,768]{1,0:T(8,128)(2,1)S(1)} collective-permute-done((bf16[128,768]{1,0:T(8,128)(2,1)}, bf16[128,768]{1,0:T(8,128)(2,1)S(1)}, u32[]{:S(2)}, u32[]{:S(2)}) %collective-permute-start.28) | collective-permute-done | bytes 196640 | tf_op jit(solution)/shard_map/ppermute | solution.py:24
  280.3 4.5 copy.152
  292.1 1.8 collective-permute-done.31
  293.9 3.8 collective-permute-done.39
  310.0 8.9 %collective-permute-done.52 = bf16[2,2,2,2,24]{4,1,0,3,2:T(2,128)(2,1)S(1)} collective-permute-done((bf16[2,2,2,2,24]{4,1,0,3,2:T(2,128)(2,1)S(1)}, bf16[2,2,2,2,24]{4,1,0,3,2:T(2,128)(2,1)S(1)}, u32[]{:S(2)}, u32[]{:S(2)}) %collective-permute-start.52) | collective-permute-done | bytes 800 | tf_op jit(solution)/shard_map/ppermute | solution.py:24
  320.4 2.1 collective-permute-done.53
  322.6 3.5 collective-permute-start.54
  328.3 3.4 collective-permute-done.40
  335.1 11.9 %attend_back.2 = (bf16[512,1920]{1,0:T(8,128)(2,1)}, f32[6,128,384]{2,1,0:T(8,128)S(1)}, f32[512,768]{1,0:T(8,128)S(1)}) custom-call(bf16[512,768]{1,0:T(8,128)(2,1)S(1)} %bitcast.422, bf16[512,1920]{1,0:T(8,128)(2,1)} %get-tuple-element.26.proj_ref, bf16[6,512,512]{2,1,0:T(8,128)(2,1)} %get-tuple-element.27.prob_ref, bf16[768,1920]{1,0:T(8,128)(2,1)} %bitcast.430, ...), custom_call_target="tpu_custom_call" | custom-call | tf_op jit(solution)/shard_map/attend_back/pallas_call | solution.py:159
  348.8 12.4 %attend_back.3 = (bf16[512,1920]{1,0:T(8,128)(2,1)}, f32[6,128,384]{2,1,0:T(8,128)S(1)}, f32[512,768]{1,0:T(8,128)S(1)}) custom-call(bf16[512,768]{1,0:T(8,128)(2,1)S(1)} %bitcast.424, bf16[512,1920]{1,0:T(8,128)(2,1)} %get-tuple-element.29.proj_ref, bf16[6,512,512]{2,1,0:T(8,128)(2,1)} %get-tuple-element.30.prob_ref, bf16[768,1920]{1,0:T(8,128)(2,1)} %bitcast.431, ...), custom_call_target="tpu_custom_call" | custom-call | tf_op jit(solution)/shard_map/attend_back/pallas_call | solution.py:159
  369.9 2.2 convolution_convert_fusion
  372.7 2.4 pad_maximum_fusion.1
  375.1 5.2 %gather_fusion.7 = bf16[8,96,2688]{2,1,0:T(8,128)(2,1)} fusion(bf16[8,96,2688]{2,1,0:T(8,128)(2,1)} %pad_maximum_fusion.1, s32[1024]{0:T(1024)} %copy-done.55), kind=kCustom, calls=%fused_computation.1.clone | custom fusion | bytes 8257568 | tf_op jit(solution)/shard_map/jit(_take)/gather | solution.py:64
  380.3 2.6 broadcast_select_fusion
  390.5 39.9 %collective-permute-done.44 = bf16[2,2,96,2688]{3,2,0,1:T(8,128)(2,1)S(1)} collective-permute-done((bf16[2,2,96,2688]{3,2,0,1:T(8,128)(2,1)S(1)}, bf16[2,2,96,2688]{3,2,0,1:T(8,128)(2,1)S(1)}, u32[]{:S(2)}, u32[]{:S(2)}) %collective-permute-start.44) | collective-permute-done | bytes 2064416 | tf_op jit(solution)/shard_map/ppermute | solution.py:24
  433.7 21.3 %collective-permute-done.45 = bf16[2,96,2688]{2,1,0:T(8,128)(2,1)S(1)} collective-permute-done((bf16[2,96,2688]{2,1,0:T(8,128)(2,1)S(1)}, bf16[2,96,2688]{2,1,0:T(8,128)(2,1)S(1)}, u32[]{:S(2)}, u32[]{:S(2)}) %collective-permute-start.45) | collective-permute-done | bytes 1032224 | tf_op jit(solution)/shard_map/ppermute | solution.py:24
  456.3 23.0 %collective-permute-done.46 = bf16[96,2688]{1,0:T(8,128)(2,1)S(1)} collective-permute-done((bf16[96,2688]{1,0:T(8,128)(2,1)S(1)}, bf16[96,2688]{1,0:T(8,128)(2,1)S(1)}, u32[]{:S(2)}, u32[]{:S(2)}) %collective-permute-start.46) | collective-permute-done | bytes 516128 | tf_op jit(solution)/shard_map/ppermute | solution.py:24
  484.9 2.5 collective-permute-done.48
  (477 shorter events, 143.2 us)
Async XLA Ops:
  1.5 76.5 %collective-permute-start.10 = (bf16[1,2,2,24]{3,2,1,0:T(2,128)(2,1)S(1)}, bf16[1,2,2,24]{3,2,1,0:T(2,128)(2,1)S(1)}, u32[]{:S(2)}, u32[]{:S(2)}) collective-permute-start(bf16[1,2,2,24]{3,2,1,0:T(2,128)(2,1)S(1)} %get-tuple-element.164), channel_id=1, source_target_pairs={{0,2},{1,3},{2,0},{3,1},{4,6},{5,7},{6,4},{7,5},{8,10},{9,11},{10,... | collective-permute-start | bytes 584 | tf_op jit(solution)/shard_map/ppermute | solution.py:24
  5.3 10.7 %collective-permute-start.4 = (bf16[3,3,16,128]{3,2,1,0:T(8,128)(2,1)S(1)}, bf16[3,3,16,128]{3,2,1,0:T(8,128)(2,1)S(1)}, u32[]{:S(2)}, u32[]{:S(2)}) collective-permute-start(bf16[3,3,16,128]{3,2,1,0:T(8,128)(2,1)S(1)} %get-tuple-element.149), channel_id=1, source_target_pairs={{0,2},{1,3},{2,0},{3,1},{4,6},{5,7},{6,4},{7,5},{8,10},{9,11},{10,... | collective-permute-start | bytes 110600 | tf_op jit(solution)/shard_map/ppermute | solution.py:24
  6.3 12.4 %collective-permute-start.3 = (bf16[96,192]{1,0:T(8,128)(2,1)S(1)}, bf16[96,192]{1,0:T(8,128)(2,1)S(1)}, u32[]{:S(2)}, u32[]{:S(2)}) collective-permute-start(bf16[96,192]{1,0:T(8,128)(2,1)S(1)} %bitcast.513), channel_id=1, source_target_pairs={{0,2},{1,3},{2,0},{3,1},{4,6},{5,7},{6,4},{7,5},{8,10},{9,11},{10,... | collective-permute-start | bytes 110600 | tf_op jit(solution)/shard_map/ppermute | solution.py:24
  9.4 8.3 %collective-permute-start.2 = (bf16[96,5,192]{2,0,1:T(8,128)(2,1)S(1)}, bf16[96,5,192]{2,0,1:T(8,128)(2,1)S(1)}, u32[]{:S(2)}, u32[]{:S(2)}) collective-permute-start(bf16[96,5,192]{2,0,1:T(8,128)(2,1)S(1)} %get-tuple-element.138), channel_id=1, source_target_pairs={{0,2},{1,3},{2,0},{3,1},{4,6},{5,7},{6,4},{7,5},{8,10},{9,11},{10,... | collective-permute-start | bytes 552968 | tf_op jit(solution)/shard_map/ppermute | solution.py:24
  10.4 146.2 %collective-permute-start.17 = (bf16[96,1536]{1,0:T(8,128)(2,1)}, bf16[96,1536]{1,0:T(8,128)(2,1)}, u32[]{:S(2)}, u32[]{:S(2)}) collective-permute-start(bf16[96,1536]{1,0:T(8,128)(2,1)} %get-tuple-element.145), channel_id=1, source_target_pairs={{0,16},{4,20},{8,24},{12,28},{16,0},{20,4},{24,8},{28,12},{1,17},{... | collective-permute-start | bytes 884744 | tf_op jit(solution)/shard_map/ppermute | solution.py:24
  16.0 34.5 %collective-permute-start = (bf16[2,2,128,768]{3,2,1,0:T(8,128)(2,1)}, bf16[2,2,128,768]{3,2,1,0:T(8,128)(2,1)S(1)}, u32[]{:S(2)}, u32[]{:S(2)}) collective-permute-start(bf16[2,2,128,768]{3,2,1,0:T(8,128)(2,1)} %pad_maximum_fusion.9), channel_id=1, source_target_pairs={{0,2},{1,3},{2,0},{3,1},{4,6},{5,7},{6,4},{7,5},{8,10},{9,11},{10,... | collective-permute-start | bytes 2359304 | tf_op jit(solution)/shard_map/ppermute | solution.py:24
  19.3 28.7 %collective-permute-start.5 = (bf16[96,2688]{1,0:T(8,128)(2,1)S(1)}, bf16[96,2688]{1,0:T(8,128)(2,1)S(1)}, u32[]{:S(2)}, u32[]{:S(2)}) collective-permute-start(bf16[96,2688]{1,0:T(8,128)(2,1)S(1)} %concatenate.123), channel_id=1, source_target_pairs={{0,16},{4,20},{8,24},{12,28},{16,0},{20,4},{24,8},{28,12},{1,17},{... | collective-permute-start | bytes 1548296 | tf_op jit(solution)/shard_map/ppermute | solution.py:24
  49.1 24.0 %collective-permute-start.6 = (bf16[2,96,2688]{2,1,0:T(8,128)(2,1)}, bf16[2,96,2688]{2,1,0:T(8,128)(2,1)}, u32[]{:S(2)}, u32[]{:S(2)}) collective-permute-start(bf16[2,96,2688]{2,1,0:T(8,128)(2,1)} %get-tuple-element.126), channel_id=1, source_target_pairs={{0,8},{4,12},{8,0},{12,4},{16,24},{20,28},{24,16},{28,20},{1,9},{5... | collective-permute-start | bytes 3096584 | tf_op jit(solution)/shard_map/ppermute | solution.py:24
  51.9 71.9 %collective-permute-start.1 = (bf16[2,2,2,128,768]{4,3,2,1,0:T(8,128)(2,1)}, bf16[2,2,2,128,768]{4,3,2,1,0:T(8,128)(2,1)}, u32[]{:S(2)}, u32[]{:S(2)}) collective-permute-start(bf16[2,2,2,128,768]{4,3,2,1,0:T(8,128)(2,1)} %pad_maximum_fusion.6), channel_id=1, source_target_pairs={{0,1},{1,0},{2,3},{3,2},{4,5},{5,4},{6,7},{7,6},{8,9},{9,8},{10,11... | collective-permute-start | bytes 4718600 | tf_op jit(solution)/shard_map/ppermute | solution.py:24
  76.6 50.9 %collective-permute-start.7 = (bf16[2,2,96,2688]{3,2,0,1:T(8,128)(2,1)}, bf16[2,2,96,2688]{3,2,0,1:T(8,128)(2,1)}, u32[]{:S(2)}, u32[]{:S(2)}) collective-permute-start(bf16[2,2,96,2688]{3,2,0,1:T(8,128)(2,1)} %get-tuple-element.120), channel_id=1, source_target_pairs={{0,4},{4,0},{8,12},{12,8},{16,20},{20,16},{24,28},{28,24},{1,5},{5... | collective-permute-start | bytes 6193160 | tf_op jit(solution)/shard_map/ppermute | solution.py:24
  80.6 5.0 %collective-permute-start.12 = (bf16[4,2,2,24]{3,2,1,0:T(2,128)(2,1)S(1)}, bf16[4,2,2,24]{3,2,1,0:T(2,128)(2,1)S(1)}, u32[]{:S(2)}, u32[]{:S(2)}) collective-permute-start(bf16[4,2,2,24]{3,2,1,0:T(2,128)(2,1)S(1)} %broadcast_select_fusion.4), channel_id=1, source_target_pairs={{0,16},{4,20},{8,24},{12,28},{16,0},{20,4},{24,8},{28,12},{1,17},{... | collective-permute-start | bytes 2312 | tf_op jit(solution)/shard_map/ppermute | solution.py:24
  89.4 33.0 %collective-permute-start.14 = (bf16[2,2,4,2,2,24]{5,4,3,2,0,1:T(2,128)(2,1)S(1)}, bf16[2,2,4,2,2,24]{5,4,3,2,0,1:T(2,128)(2,1)S(1)}, u32[]{:S(2)}, u32[]{:S(2)}) collective-permute-start(bf16[2,2,4,2,2,24]{5,4,3,2,0,1:T(2,128)(2,1)S(1)} %pad_maximum_fusion.28), channel_id=1, source_target_pairs={{0,4},{4,0},{8,12},{12,8},{16,20},{20,16},{24,28},{28,24},{1,5},{5... | collective-permute-start | bytes 9224 | tf_op jit(solution)/shard_map/ppermute | solution.py:24
  156.3 15.9 %collective-permute-start.8 = (bf16[2,128,768]{2,1,0:T(8,128)(2,1)}, bf16[2,128,768]{2,1,0:T(8,128)(2,1)}, u32[]{:S(2)}, u32[]{:S(2)}) collective-permute-start(bf16[2,128,768]{2,1,0:T(8,128)(2,1)} %bitcast.37), channel_id=1, source_target_pairs={{0,1},{1,0},{2,3},{3,2},{4,5},{5,4},{6,7},{7,6},{8,9},{9,8},{10,11... | collective-permute-start | bytes 1179656 | tf_op jit(solution)/shard_map/ppermute | solution.py:24
  157.9 17.6 %collective-permute-start.18 = (bf16[2,96,1536]{2,1,0:T(8,128)(2,1)S(1)}, bf16[2,96,1536]{2,1,0:T(8,128)(2,1)S(1)}, u32[]{:S(2)}, u32[]{:S(2)}) collective-permute-start(bf16[2,96,1536]{2,1,0:T(8,128)(2,1)S(1)} %get-tuple-element.136), channel_id=1, source_target_pairs={{0,8},{4,12},{8,0},{12,4},{16,24},{20,28},{24,16},{28,20},{1,9},{5... | collective-permute-start | bytes 1769480 | tf_op jit(solution)/shard_map/ppermute | solution.py:24
  173.3 7.8 %collective-permute-start.9 = (bf16[128,768]{1,0:T(8,128)(2,1)S(1)}, bf16[128,768]{1,0:T(8,128)(2,1)S(1)}, u32[]{:S(2)}, u32[]{:S(2)}) collective-permute-start(bf16[128,768]{1,0:T(8,128)(2,1)S(1)} %fusion.55), channel_id=1, source_target_pairs={{0,2},{1,3},{2,0},{3,1},{4,6},{5,7},{6,4},{7,5},{8,10},{9,11},{10,... | collective-permute-start | bytes 589832 | tf_op jit(solution)/shard_map/ppermute | solution.py:24
  175.0 9.7 %collective-permute-start.23 = (bf16[128,768]{1,0:T(8,128)(2,1)S(1)}, bf16[128,768]{1,0:T(8,128)(2,1)S(1)}, u32[]{:S(2)}, u32[]{:S(2)}) collective-permute-start(bf16[128,768]{1,0:T(8,128)(2,1)S(1)} %fusion.57), channel_id=1, source_target_pairs={{0,2},{1,3},{2,0},{3,1},{4,6},{5,7},{6,4},{7,5},{8,10},{9,11},{10,... | collective-permute-start | bytes 589832 | tf_op jit(solution)/shard_map/ppermute | solution.py:24
  175.7 27.7 %collective-permute-start.19 = (bf16[2,2,96,1536]{3,2,1,0:T(8,128)(2,1)S(1)}, bf16[2,2,96,1536]{3,2,1,0:T(8,128)(2,1)S(1)}, u32[]{:S(2)}, u32[]{:S(2)}) collective-permute-start(bf16[2,2,96,1536]{3,2,1,0:T(8,128)(2,1)S(1)} %get-tuple-element.122), channel_id=1, source_target_pairs={{0,4},{4,0},{8,12},{12,8},{16,20},{20,16},{24,28},{28,24},{1,5},{5... | collective-permute-start | bytes 3538952 | tf_op jit(solution)/shard_map/ppermute | solution.py:24
  185.3 6.4 %collective-permute-start.15 = (bf16[128,768]{1,0:T(8,128)(2,1)S(1)}, bf16[128,768]{1,0:T(8,128)(2,1)S(1)}, u32[]{:S(2)}, u32[]{:S(2)}) collective-permute-start(bf16[128,768]{1,0:T(8,128)(2,1)S(1)} %fusion.50), channel_id=1, source_target_pairs={{0,2},{1,3},{2,0},{3,1},{4,6},{5,7},{6,4},{7,5},{8,10},{9,11},{10,... | collective-permute-start | bytes 589832 | tf_op jit(solution)/shard_map/ppermute | solution.py:24
  191.7 12.1 %collective-permute-start.16 = (bf16[2,128,768]{2,1,0:T(8,128)(2,1)S(1)}, bf16[2,128,768]{2,1,0:T(8,128)(2,1)S(1)}, u32[]{:S(2)}, u32[]{:S(2)}) collective-permute-start(bf16[2,128,768]{2,1,0:T(8,128)(2,1)S(1)} %pad_maximum_fusion.19), channel_id=1, source_target_pairs={{0,1},{1,0},{2,3},{3,2},{4,5},{5,4},{6,7},{7,6},{8,9},{9,8},{10,11... | collective-permute-start | bytes 1179656 | tf_op jit(solution)/shard_map/ppermute | solution.py:24
  208.8 7.0 %collective-permute-start.21 = (bf16[128,768]{1,0:T(8,128)(2,1)S(1)}, bf16[128,768]{1,0:T(8,128)(2,1)S(1)}, u32[]{:S(2)}, u32[]{:S(2)}) collective-permute-start(bf16[128,768]{1,0:T(8,128)(2,1)S(1)} %fusion.56), channel_id=1, source_target_pairs={{0,2},{1,3},{2,0},{3,1},{4,6},{5,7},{6,4},{7,5},{8,10},{9,11},{10,... | collective-permute-start | bytes 589832 | tf_op jit(solution)/shard_map/ppermute | solution.py:24
  216.1 6.2 %collective-permute-start.24 = (bf16[128,768]{1,0:T(8,128)(2,1)S(1)}, bf16[128,768]{1,0:T(8,128)(2,1)S(1)}, u32[]{:S(2)}, u32[]{:S(2)}) collective-permute-start(bf16[128,768]{1,0:T(8,128)(2,1)S(1)} %get-tuple-element.154), channel_id=1, source_target_pairs={{0,2},{1,3},{2,0},{3,1},{4,6},{5,7},{6,4},{7,5},{8,10},{9,11},{10,... | collective-permute-start | bytes 589832 | tf_op jit(solution)/shard_map/ppermute | solution.py:24
  230.3 8.2 %collective-permute-start.26 = (bf16[2,128,768]{2,1,0:T(8,128)(2,1)S(1)}, bf16[2,128,768]{2,1,0:T(8,128)(2,1)}, u32[]{:S(2)}, u32[]{:S(2)}) collective-permute-start(bf16[2,128,768]{2,1,0:T(8,128)(2,1)S(1)} %bitcast.502), channel_id=1, source_target_pairs={{0,1},{1,0},{2,3},{3,2},{4,5},{5,4},{6,7},{7,6},{8,9},{9,8},{10,11... | collective-permute-start | bytes 1179656 | tf_op jit(solution)/shard_map/ppermute | solution.py:24
  240.5 7.0 %collective-permute-start.27 = (bf16[128,768]{1,0:T(8,128)(2,1)S(1)}, bf16[128,768]{1,0:T(8,128)(2,1)S(1)}, u32[]{:S(2)}, u32[]{:S(2)}) collective-permute-start(bf16[128,768]{1,0:T(8,128)(2,1)S(1)} %fusion.58), channel_id=1, source_target_pairs={{0,2},{1,3},{2,0},{3,1},{4,6},{5,7},{6,4},{7,5},{8,10},{9,11},{10,... | collective-permute-start | bytes 589832 | tf_op jit(solution)/shard_map/ppermute | solution.py:24
  249.1 6.2 %collective-permute-start.36 = (bf16[128,768]{1,0:T(8,128)(2,1)S(1)}, bf16[128,768]{1,0:T(8,128)(2,1)S(1)}, u32[]{:S(2)}, u32[]{:S(2)}) collective-permute-start(bf16[128,768]{1,0:T(8,128)(2,1)S(1)} %add_convert_fusion.5), channel_id=1, source_target_pairs={{0,2},{1,3},{2,0},{3,1},{4,6},{5,7},{6,4},{7,5},{8,10},{9,11},{10,... | collective-permute-start | bytes 589832 | tf_op jit(solution)/shard_map/ppermute | solution.py:24
  256.1 8.7 %collective-permute-start.37 = (bf16[2,128,768]{2,1,0:T(8,128)(2,1)}, bf16[2,128,768]{2,1,0:T(8,128)(2,1)}, u32[]{:S(2)}, u32[]{:S(2)}) collective-permute-start(bf16[2,128,768]{2,1,0:T(8,128)(2,1)} %pad_maximum_fusion.24), channel_id=1, source_target_pairs={{0,1},{1,0},{2,3},{3,2},{4,5},{5,4},{6,7},{7,6},{8,9},{9,8},{10,11... | collective-permute-start | bytes 1179656 | tf_op jit(solution)/shard_map/ppermute | solution.py:24
  257.1 7.6 %collective-permute-start.28 = (bf16[128,768]{1,0:T(8,128)(2,1)}, bf16[128,768]{1,0:T(8,128)(2,1)S(1)}, u32[]{:S(2)}, u32[]{:S(2)}) collective-permute-start(bf16[128,768]{1,0:T(8,128)(2,1)} %add_convert_fusion.6), channel_id=1, source_target_pairs={{0,2},{1,3},{2,0},{3,1},{4,6},{5,7},{6,4},{7,5},{8,10},{9,11},{10,... | collective-permute-start | bytes 589832 | tf_op jit(solution)/shard_map/ppermute | solution.py:24
  264.7 5.8 %collective-permute-start.29 = (bf16[2,128,768]{2,1,0:T(8,128)(2,1)S(1)}, bf16[2,128,768]{2,1,0:T(8,128)(2,1)S(1)}, u32[]{:S(2)}, u32[]{:S(2)}) collective-permute-start(bf16[2,128,768]{2,1,0:T(8,128)(2,1)S(1)} %pad_maximum_fusion.22), channel_id=1, source_target_pairs={{0,1},{1,0},{2,3},{3,2},{4,5},{5,4},{6,7},{7,6},{8,9},{9,8},{10,11... | collective-permute-start | bytes 1179656 | tf_op jit(solution)/shard_map/ppermute | solution.py:24
  277.2 7.6 %collective-permute-start.30 = (bf16[2,128,768]{2,1,0:T(8,128)(2,1)S(1)}, bf16[2,128,768]{2,1,0:T(8,128)(2,1)}, u32[]{:S(2)}, u32[]{:S(2)}) collective-permute-start(bf16[2,128,768]{2,1,0:T(8,128)(2,1)S(1)} %bitcast.501), channel_id=1, source_target_pairs={{0,1},{1,0},{2,3},{3,2},{4,5},{5,4},{6,7},{7,6},{8,9},{9,8},{10,11... | collective-permute-start | bytes 1179656 | tf_op jit(solution)/shard_map/ppermute | solution.py:24
  277.7 10.0 %collective-permute-start.38 = (bf16[2,128,768]{2,1,0:T(8,128)(2,1)}, bf16[2,128,768]{2,1,0:T(8,128)(2,1)}, u32[]{:S(2)}, u32[]{:S(2)}) collective-permute-start(bf16[2,128,768]{2,1,0:T(8,128)(2,1)} %bitcast.119), channel_id=1, source_target_pairs={{0,1},{1,0},{2,3},{3,2},{4,5},{5,4},{6,7},{7,6},{8,9},{9,8},{10,11... | collective-permute-start | bytes 1179656 | tf_op jit(solution)/shard_map/ppermute | solution.py:24
  286.2 7.8 %collective-permute-start.31 = (bf16[128,768]{1,0:T(8,128)(2,1)S(1)}, bf16[128,768]{1,0:T(8,128)(2,1)S(1)}, u32[]{:S(2)}, u32[]{:S(2)}) collective-permute-start(bf16[128,768]{1,0:T(8,128)(2,1)S(1)} %fusion.59), channel_id=1, source_target_pairs={{0,2},{1,3},{2,0},{3,1},{4,6},{5,7},{6,4},{7,5},{8,10},{9,11},{10,... | collective-permute-start | bytes 589832 | tf_op jit(solution)/shard_map/ppermute | solution.py:24
  288.8 8.9 %collective-permute-start.39 = (bf16[128,768]{1,0:T(8,128)(2,1)S(1)}, bf16[128,768]{1,0:T(8,128)(2,1)S(1)}, u32[]{:S(2)}, u32[]{:S(2)}) collective-permute-start(bf16[128,768]{1,0:T(8,128)(2,1)S(1)} %fusion.61), channel_id=1, source_target_pairs={{0,2},{1,3},{2,0},{3,1},{4,6},{5,7},{6,4},{7,5},{8,10},{9,11},{10,... | collective-permute-start | bytes 589832 | tf_op jit(solution)/shard_map/ppermute | solution.py:24
  290.6 41.2 %collective-permute-start.55 = (bf16[2,2,96,1536]{3,2,1,0:T(8,128)(2,1)}, bf16[2,2,96,1536]{3,2,1,0:T(8,128)(2,1)}, u32[]{:S(2)}, u32[]{:S(2)}) collective-permute-start(bf16[2,2,96,1536]{3,2,1,0:T(8,128)(2,1)} %slice_bitcast_fusion.8), channel_id=1, source_target_pairs={{0,4},{4,0},{8,12},{12,8},{16,20},{20,16},{24,28},{28,24},{1,5},{5... | collective-permute-start | bytes 3538952 | tf_op jit(solution)/shard_map/ppermute | solution.py:24
  306.9 12.0 %collective-permute-start.52 = (bf16[2,2,2,2,24]{4,1,0,3,2:T(2,128)(2,1)S(1)}, bf16[2,2,2,2,24]{4,1,0,3,2:T(2,128)(2,1)S(1)}, u32[]{:S(2)}, u32[]{:S(2)}) collective-permute-start(bf16[2,2,2,2,24]{4,1,0,3,2:T(2,128)(2,1)S(1)} %bitcast.522), channel_id=1, source_target_pairs={{0,4},{4,0},{8,12},{12,8},{16,20},{20,16},{24,28},{28,24},{1,5},{5... | collective-permute-start | bytes 2312 | tf_op jit(solution)/shard_map/ppermute | solution.py:24
  308.5 19.7 %collective-permute-start.32 = (bf16[128,768]{1,0:T(8,128)(2,1)S(1)}, bf16[128,768]{1,0:T(8,128)(2,1)S(1)}, u32[]{:S(2)}, u32[]{:S(2)}) collective-permute-start(bf16[128,768]{1,0:T(8,128)(2,1)S(1)} %get-tuple-element.83), channel_id=1, source_target_pairs={{0,2},{1,3},{2,0},{3,1},{4,6},{5,7},{6,4},{7,5},{8,10},{9,11},{10,... | collective-permute-start | bytes 589832 | tf_op jit(solution)/shard_map/ppermute | solution.py:24
  326.0 5.7 %collective-permute-start.40 = (bf16[128,768]{1,0:T(8,128)(2,1)S(1)}, bf16[128,768]{1,0:T(8,128)(2,1)S(1)}, u32[]{:S(2)}, u32[]{:S(2)}) collective-permute-start(bf16[128,768]{1,0:T(8,128)(2,1)S(1)} %get-tuple-element.90), channel_id=1, source_target_pairs={{0,2},{1,3},{2,0},{3,1},{4,6},{5,7},{6,4},{7,5},{8,10},{9,11},{10,... | collective-permute-start | bytes 589832 | tf_op jit(solution)/shard_map/ppermute | solution.py:24
  328.2 6.8 %collective-permute-start.33 = (bf16[2,128,768]{2,1,0:T(8,128)(2,1)S(1)}, bf16[2,128,768]{2,1,0:T(8,128)(2,1)S(1)}, u32[]{:S(2)}, u32[]{:S(2)}) collective-permute-start(bf16[2,128,768]{2,1,0:T(8,128)(2,1)S(1)} %pad_maximum_fusion.23), channel_id=1, source_target_pairs={{0,1},{1,0},{2,3},{3,2},{4,5},{5,4},{6,7},{7,6},{8,9},{9,8},{10,11... | collective-permute-start | bytes 1179656 | tf_op jit(solution)/shard_map/ppermute | solution.py:24
  331.7 17.0 %collective-permute-start.41 = (bf16[2,128,768]{2,1,0:T(8,128)(2,1)S(1)}, bf16[2,128,768]{2,1,0:T(8,128)(2,1)S(1)}, u32[]{:S(2)}, u32[]{:S(2)}) collective-permute-start(bf16[2,128,768]{2,1,0:T(8,128)(2,1)S(1)} %pad_maximum_fusion.25), channel_id=1, source_target_pairs={{0,1},{1,0},{2,3},{3,2},{4,5},{5,4},{6,7},{7,6},{8,9},{9,8},{10,11... | collective-permute-start | bytes 1179656 | tf_op jit(solution)/shard_map/ppermute | solution.py:24
  334.4 54.1 %collective-permute-start.56 = (bf16[2,96,1536]{2,1,0:T(8,128)(2,1)}, bf16[2,96,1536]{2,1,0:T(8,128)(2,1)}, u32[]{:S(2)}, u32[]{:S(2)}) collective-permute-start(bf16[2,96,1536]{2,1,0:T(8,128)(2,1)} %fusion.23), channel_id=1, source_target_pairs={{0,8},{4,12},{8,0},{12,4},{16,24},{20,28},{24,16},{28,20},{1,9},{5... | collective-permute-start | bytes 1769480 | tf_op jit(solution)/shard_map/ppermute | solution.py:24
  362.9 22.1 %collective-permute-start.34 = (bf16[2,128,768]{2,1,0:T(8,128)(2,1)}, bf16[2,128,768]{2,1,0:T(8,128)(2,1)}, u32[]{:S(2)}, u32[]{:S(2)}) collective-permute-start(bf16[2,128,768]{2,1,0:T(8,128)(2,1)} %bitcast.109), channel_id=1, source_target_pairs={{0,1},{1,0},{2,3},{3,2},{4,5},{5,4},{6,7},{7,6},{8,9},{9,8},{10,11... | collective-permute-start | bytes 1179656 | tf_op jit(solution)/shard_map/ppermute | solution.py:24
  364.2 23.4 %collective-permute-start.42 = (bf16[2,128,768]{2,1,0:T(8,128)(2,1)}, bf16[2,128,768]{2,1,0:T(8,128)(2,1)S(1)}, u32[]{:S(2)}, u32[]{:S(2)}) collective-permute-start(bf16[2,128,768]{2,1,0:T(8,128)(2,1)} %bitcast.127), channel_id=1, source_target_pairs={{0,1},{1,0},{2,3},{3,2},{4,5},{5,4},{6,7},{7,6},{8,9},{9,8},{10,11... | collective-permute-start | bytes 1179656 | tf_op jit(solution)/shard_map/ppermute | solution.py:24
  383.5 47.0 %collective-permute-start.44 = (bf16[2,2,96,2688]{3,2,0,1:T(8,128)(2,1)S(1)}, bf16[2,2,96,2688]{3,2,0,1:T(8,128)(2,1)S(1)}, u32[]{:S(2)}, u32[]{:S(2)}) collective-permute-start(bf16[2,2,96,2688]{3,2,0,1:T(8,128)(2,1)S(1)} %bitcast.464), channel_id=1, source_target_pairs={{0,4},{4,0},{8,12},{12,8},{16,20},{20,16},{24,28},{28,24},{1,5},{5... | collective-permute-start | bytes 6193160 | tf_op jit(solution)/shard_map/ppermute | solution.py:24
  386.1 46.4 %collective-permute-start.35 = (bf16[128,768]{1,0:T(8,128)(2,1)S(1)}, bf16[128,768]{1,0:T(8,128)(2,1)S(1)}, u32[]{:S(2)}, u32[]{:S(2)}) collective-permute-start(bf16[128,768]{1,0:T(8,128)(2,1)S(1)} %fusion.60), channel_id=1, source_target_pairs={{0,2},{1,3},{2,0},{3,1},{4,6},{5,7},{6,4},{7,5},{8,10},{9,11},{10,... | collective-permute-start | bytes 589832 | tf_op jit(solution)/shard_map/ppermute | solution.py:24
  387.7 44.9 %collective-permute-start.43 = (bf16[128,768]{1,0:T(8,128)(2,1)S(1)}, bf16[128,768]{1,0:T(8,128)(2,1)S(1)}, u32[]{:S(2)}, u32[]{:S(2)}) collective-permute-start(bf16[128,768]{1,0:T(8,128)(2,1)S(1)} %fusion.62), channel_id=1, source_target_pairs={{0,2},{1,3},{2,0},{3,1},{4,6},{5,7},{6,4},{7,5},{8,10},{9,11},{10,... | collective-permute-start | bytes 589832 | tf_op jit(solution)/shard_map/ppermute | solution.py:24
  390.5 65.0 %collective-permute-start.57 = (bf16[96,1536]{1,0:T(8,128)(2,1)S(1)}, bf16[96,1536]{1,0:T(8,128)(2,1)S(1)}, u32[]{:S(2)}, u32[]{:S(2)}) collective-permute-start(bf16[96,1536]{1,0:T(8,128)(2,1)S(1)} %fusion.52), channel_id=1, source_target_pairs={{0,16},{4,20},{8,24},{12,28},{16,0},{20,4},{24,8},{28,12},{1,17},{... | collective-permute-start | bytes 884744 | tf_op jit(solution)/shard_map/ppermute | solution.py:24
  431.0 24.0 %collective-permute-start.45 = (bf16[2,96,2688]{2,1,0:T(8,128)(2,1)S(1)}, bf16[2,96,2688]{2,1,0:T(8,128)(2,1)S(1)}, u32[]{:S(2)}, u32[]{:S(2)}) collective-permute-start(bf16[2,96,2688]{2,1,0:T(8,128)(2,1)S(1)} %fusion.17), channel_id=1, source_target_pairs={{0,8},{4,12},{8,0},{12,4},{16,24},{20,28},{24,16},{28,20},{1,9},{5... | collective-permute-start | bytes 3096584 | tf_op jit(solution)/shard_map/ppermute | solution.py:24
  455.3 24.0 %collective-permute-start.46 = (bf16[96,2688]{1,0:T(8,128)(2,1)S(1)}, bf16[96,2688]{1,0:T(8,128)(2,1)S(1)}, u32[]{:S(2)}, u32[]{:S(2)}) collective-permute-start(bf16[96,2688]{1,0:T(8,128)(2,1)S(1)} %fusion.25), channel_id=1, source_target_pairs={{0,16},{4,20},{8,24},{12,28},{16,0},{20,4},{24,8},{28,12},{1,17},{... | collective-permute-start | bytes 1548296 | tf_op jit(solution)/shard_map/ppermute | solution.py:24
  479.6 5.3 %collective-permute-start.49 = (bf16[192,96]{1,0:T(8,128)(2,1)S(1)}, bf16[192,96]{1,0:T(8,128)(2,1)S(1)}, u32[]{:S(2)}, u32[]{:S(2)}) collective-permute-start(bf16[192,96]{1,0:T(8,128)(2,1)S(1)} %fusion.64), channel_id=1, source_target_pairs={{0,2},{1,3},{2,0},{3,1},{4,6},{5,7},{6,4},{7,5},{8,10},{9,11},{10,... | collective-permute-start | bytes 110600 | tf_op jit(solution)/shard_map/ppermute | solution.py:24
  483.6 6.5 %collective-permute-start.47 = (bf16[5,96,192]{2,1,0:T(8,128)(2,1)S(1)}, bf16[5,96,192]{2,1,0:T(8,128)(2,1)S(1)}, u32[]{:S(2)}, u32[]{:S(2)}) collective-permute-start(bf16[5,96,192]{2,1,0:T(8,128)(2,1)S(1)} %bitcast.507), channel_id=1, source_target_pairs={{0,2},{1,3},{2,0},{3,1},{4,6},{5,7},{6,4},{7,5},{8,10},{9,11},{10,... | collective-permute-start | bytes 552968 | tf_op jit(solution)/shard_map/ppermute | solution.py:24
  (78 other events, 1083.8 us)
